TPU v7x, 32 devices: a whole 2x2x4 slice. The times are simulated.
32 devices in a mesh: wrow: 16 (over z, y, x), kblk: 2 (over core).
Axes of the slice: x: 2, y: 2, z: 4, core: 2. Of those that a mesh axis runs over, the one named last changes fastest.
Arguments:
- conduction: bfloat16 [2, 4, 64, 16384], P('kblk', None, None, 'wrow'), may hold values from -6 to 6
- valence: bfloat16 [2, 4, 64, 16384], P(None, None, 'wrow', 'kblk'), may hold values from -6 to 6
- screened: bfloat16 [4, 16384, 16384], P(None, 'wrow', 'kblk'), may hold values from -0.00036621094 to 0.00036621094
- pair_block: int32 [2, 4], replicated, may hold values from 0 to 3, as said below
Outputs:
- kernel: float32 [2, 64, 256], P('kblk', 'wrow')
Inputs may be any that keep to these rules, and one draw needn't show every extreme that they name: `pair_block`: every one of the 4 blocks is selected by at least one pair and by at most 3 pairs; one block by exactly 3 pairs.
All inputs are finite; a program needn't handle non-finite values.
Results may differ from a plain program's by a relative error of at most 0.0029.
Values may be sent and summed in bfloat16 or wider, within the bound.
No kernel may reach another device: no remote copies, remote signals or barrier semaphores. Data moves between devices by JAX's collectives and lax.ppermute only.
A program may use at most 128 MiB of HBM per device.

v0:
```python
import jax
import jax.numpy as jnp
from jax import lax
from jax.sharding import PartitionSpec as P

C = 8
V = 8


def per_device(conduction, valence, screened, pair_block):
    gathered_cond = lax.all_gather(conduction, "kblk", axis=0, tiled=True)
    gathered_vale = lax.all_gather(valence, "wrow", axis=2, tiled=True)
    k_count = gathered_cond.shape[0]
    kp_count = gathered_cond.shape[1]
    pair_count = k_count * kp_count
    row_width = gathered_cond.shape[3]
    col_width = gathered_vale.shape[3]
    cond_flat = gathered_cond.reshape(pair_count, C * C, row_width)
    vale_flat = gathered_vale.reshape(pair_count, V * V, col_width)
    flat_blocks = pair_block.reshape(pair_count)
    pair_ids = jnp.arange(pair_count, dtype=jnp.int32)
    capacity = 3 * pair_count // 8
    block_count = screened.shape[0]

    def one_block(block, total):
        sort_keys = jnp.where(flat_blocks == block, 0, pair_count) + pair_ids
        chosen = jnp.argsort(sort_keys)[:capacity]
        present = (flat_blocks[chosen] == block).astype(jnp.float32)
        vale_sel = jnp.take(vale_flat, chosen, axis=0)
        cond_sel = jnp.take(cond_flat, chosen, axis=0)
        w_tile = lax.dynamic_index_in_dim(screened, block, 0, keepdims=False)
        screened_vale = jnp.einsum(
            "pvh,gh->pvg", vale_sel, w_tile, preferred_element_type=jnp.float32
        ).astype(jnp.bfloat16)
        tiles = jnp.einsum(
            "pcg,pvg->pcv", cond_sel, screened_vale, preferred_element_type=jnp.float32
        )
        placer = (pair_ids[:, None] == chosen[None, :]).astype(jnp.float32) * present[None, :]
        return total + jnp.einsum("sp,pcv->scv", placer, tiles, precision=lax.Precision.HIGHEST)

    terms = lax.fori_loop(
        0, block_count, one_block, jnp.zeros((pair_count, C * C, V * V), jnp.float32)
    )
    terms = terms.reshape(k_count, kp_count, C, C, V, V).transpose(0, 2, 4, 1, 3, 5)
    terms = terms.reshape(k_count, C * V, kp_count * C * V)
    by_block = lax.psum_scatter(terms, "kblk", scatter_dimension=0, tiled=True)
    return lax.psum_scatter(by_block, "wrow", scatter_dimension=1, tiled=True)


def solution(mesh):
    return jax.shard_map(
        per_device,
        mesh=mesh,
        in_specs=(
            P("kblk", None, None, "wrow"),
            P(None, None, "wrow", "kblk"),
            P(None, "wrow", "kblk"),
            P(),
        ),
        out_specs=P("kblk", "wrow", None),
        check_vma=False,
    )
```

profile of v0, /device:TPU:0, one launch (start us, length us, event | category | flops | bytes accessed | tf_op | source)
XLA Modules:
  0.0 346.6 jit_solution(13563379429917125649)
XLA Ops:
  6.5 2.2 copy.8
  10.4 114.8 %all-gather.5.cloned.1.call-done = bf16[2,4,64,8192]{3,1,0,2:T(4,128)(2,1)} async-done(((bf16[2,4,4,8192]{3,1,0,2:T(4,128)(2,1)}), bf16[2,4,64,8192]{3,1,0,2:T(4,128)(2,1)}) %all-gather.5.cloned.1.call-update) | async-done | bytes 8388624 | tf_op jit(solution)/shard_map/all_gather | solution.py:12
  125.2 11.2 %copy.11 = bf16[2,4,64,8192]{3,2,1,0:T(8,128)(2,1)} copy(bf16[2,4,64,8192]{3,1,0,2:T(4,128)(2,1)} %all-gather.5.cloned.1.call-done) | data formatting | bytes 16777216
  136.3 78.8 %while.15 = (s32[]{:T(128)}, f32[8,64,64]{2,0,1:T(8,128)S(1)}, s32[8]{0:T(128)S(1)}, bf16[8,64,1024]{2,1,0:T(8,128)(2,1)}, bf16[8,64,8192]{2,1,0:T(8,128)(2,1)},...) while((s32[]{:T(128)}, f32[8,64,64]{2,0,1:T(8,128)S(1)}, s32[8]{0:T(128)S(1)}, ...), condition=%wide.region_2.3_spmd.clone.clone, body=%wide.region_0.2_spmd.clone.clone.sunk | while | flops 3249603584 | bytes 28546016 | solution.py:41
  137.3 4.1 %gather_fusion = bf16[3,64,8192]{2,1,0:T(8,128)(2,1)S(1)} fusion(bf16[8,64,8192]{2,1,0:T(8,128)(2,1)} %get-tuple-element.260, s32[1024]{0:T(1024)S(1)} %pad_clamp_fusion.2), kind=kCustom, calls=%fused_computation.2.clone.clone.1 | custom fusion | bytes 6291468 | tf_op jit(solution)/shard_map/while/body/eval_jaxpr/jit(_take)/gather | solution.py:29
  141.5 10.3 %fusion.45 = bf16[3,64,1024]{2,1,0:T(8,128)(2,1)} fusion(bf16[4,1024,8192]{2,1,0:T(8,128)(2,1)} %get-tuple-element.261, s32[]{:T(128)} %get-tuple-element.248, bf16[3,64,8192]{2,1,0:T(8,128)(2,1)S(1)} %gather_fusion, pred[3]{0:T(512)(128)(4,1)S(1)} %get-tuple-element.239), kind=kOutput, calls=%fused_computation.10.clone.1 | convolution fusion | flops 3222994944 | bytes 20316676 | tf_op jit(solution)/shard_map/while/body/eval_jaxpr/pvh,gh->pvg/dot_general | solution.py:32
  151.8 1.8 gather_fusion.1
  153.6 1.3 fusion.46
  157.1 4.1 %gather_fusion = bf16[3,64,8192]{2,1,0:T(8,128)(2,1)S(1)} fusion(bf16[8,64,8192]{2,1,0:T(8,128)(2,1)} %get-tuple-element.260, s32[1024]{0:T(1024)S(1)} %pad_clamp_fusion.2), kind=kCustom, calls=%fused_computation.2.clone.clone.1 | custom fusion | bytes 6291468 | tf_op jit(solution)/shard_map/while/body/eval_jaxpr/jit(_take)/gather | solution.py:29
  161.2 10.3 %fusion.45 = bf16[3,64,1024]{2,1,0:T(8,128)(2,1)} fusion(bf16[4,1024,8192]{2,1,0:T(8,128)(2,1)} %get-tuple-element.261, s32[]{:T(128)} %get-tuple-element.248, bf16[3,64,8192]{2,1,0:T(8,128)(2,1)S(1)} %gather_fusion, pred[3]{0:T(512)(128)(4,1)S(1)} %get-tuple-element.239), kind=kOutput, calls=%fused_computation.10.clone.1 | convolution fusion | flops 3222994944 | bytes 20316676 | tf_op jit(solution)/shard_map/while/body/eval_jaxpr/pvh,gh->pvg/dot_general | solution.py:32
  171.5 1.8 gather_fusion.1
  173.3 1.3 fusion.46
  176.8 4.1 %gather_fusion = bf16[3,64,8192]{2,1,0:T(8,128)(2,1)S(1)} fusion(bf16[8,64,8192]{2,1,0:T(8,128)(2,1)} %get-tuple-element.260, s32[1024]{0:T(1024)S(1)} %pad_clamp_fusion.2), kind=kCustom, calls=%fused_computation.2.clone.clone.1 | custom fusion | bytes 6291468 | tf_op jit(solution)/shard_map/while/body/eval_jaxpr/jit(_take)/gather | solution.py:29
  180.9 10.3 %fusion.45 = bf16[3,64,1024]{2,1,0:T(8,128)(2,1)} fusion(bf16[4,1024,8192]{2,1,0:T(8,128)(2,1)} %get-tuple-element.261, s32[]{:T(128)} %get-tuple-element.248, bf16[3,64,8192]{2,1,0:T(8,128)(2,1)S(1)} %gather_fusion, pred[3]{0:T(512)(128)(4,1)S(1)} %get-tuple-element.239), kind=kOutput, calls=%fused_computation.10.clone.1 | convolution fusion | flops 3222994944 | bytes 20316676 | tf_op jit(solution)/shard_map/while/body/eval_jaxpr/pvh,gh->pvg/dot_general | solution.py:32
  191.2 1.8 gather_fusion.1
  193.0 1.3 fusion.46
  196.5 4.1 %gather_fusion = bf16[3,64,8192]{2,1,0:T(8,128)(2,1)S(1)} fusion(bf16[8,64,8192]{2,1,0:T(8,128)(2,1)} %get-tuple-element.260, s32[1024]{0:T(1024)S(1)} %pad_clamp_fusion.2), kind=kCustom, calls=%fused_computation.2.clone.clone.1 | custom fusion | bytes 6291468 | tf_op jit(solution)/shard_map/while/body/eval_jaxpr/jit(_take)/gather | solution.py:29
  200.6 10.3 %fusion.45 = bf16[3,64,1024]{2,1,0:T(8,128)(2,1)} fusion(bf16[4,1024,8192]{2,1,0:T(8,128)(2,1)} %get-tuple-element.261, s32[]{:T(128)} %get-tuple-element.248, bf16[3,64,8192]{2,1,0:T(8,128)(2,1)S(1)} %gather_fusion, pred[3]{0:T(512)(128)(4,1)S(1)} %get-tuple-element.239), kind=kOutput, calls=%fused_computation.10.clone.1 | convolution fusion | flops 3222994944 | bytes 20316676 | tf_op jit(solution)/shard_map/while/body/eval_jaxpr/pvh,gh->pvg/dot_general | solution.py:32
  210.9 1.8 gather_fusion.1
  212.7 1.3 fusion.46
  215.8 3.0 copy.17
  218.8 3.5 reshape.32
  222.3 6.4 %reduce-scatter.3.cloned.1.call-done = f32[1,64,256]{2,1,0:T(8,128)} async-done(((f32[2,64,256]{2,1,0:T(8,128)}), f32[1,64,256]{2,1,0:T(8,128)}) %reduce-scatter.3.cloned.1.call-update) | async-done | bytes 65552 | tf_op jit(solution)/shard_map/reduce_scatter | solution.py:46
  230.0 108.7 %all-reduce.3.cloned.1.call-done = f32[1,64,256]{2,1,0:T(8,128)} async-done(((f32[1,64,256]{2,1,0:T(8,128)}), f32[1,64,256]{2,1,0:T(8,128)}) %all-reduce.3.cloned.1.call-update) | async-done | bytes 65552
  (48 shorter events, 12.7 us)
Async XLA Ops:
  6.5 118.6 %all-gather.5.cloned.1.call-start = ((), (), s32[]{:S(2)}) async-start(), calls=%async_computation.2 | async-start | bytes 8912896 | tf_op jit(solution)/shard_map/all_gather | solution.py:12
  8.8 127.6 %all-gather.3.cloned.1.call-start = ((), (), s32[]{:S(2)}) async-start(), calls=%async_computation.1 | async-start | bytes 1572864 | tf_op jit(solution)/shard_map/all_gather | solution.py:11
  9.5 219.2 %reduce-scatter.3.cloned.1.call-start = ((), (), s32[]{:S(2)}) async-start(), calls=%async_computation.3 | async-start | bytes 196608 | tf_op jit(solution)/shard_map/reduce_scatter | solution.py:46
  215.8 13.0 %copy-start = (u32[32]{0:T(128)S(1)}, u32[32]{0:T(128)}, u32[]{:S(2)}) copy-start(u32[32]{0:T(128)} %constant.81) | copy-start | bytes 388
  222.2 116.5 %all-reduce.3.cloned.1.call-start = ((), (), s32[]{:S(2)}) async-start(), calls=%async_computation.4 | async-start | bytes 131072
Sparse Core Ops, SparseCore 0:
  10.1 115.0 all-gather.4
  126.7 7.1 all-gather.2
  222.4 6.3 reduce-scatter.2
  234.1 104.6 all-reduce.2
where the time goes:
time: 347 us
  waiting for transfers between devices  231 us (67%)
  local copies, waits for them, and re-layouts  49.3 us (14%)
  matrix products  48.4 us (14%)
  between operations  13.8 us (4%)
  other arithmetic  3.96 us (1%)
    all_gather x1, waiting for transfers between devices, per_device(): gathered_vale = lax.all_gather(valence, 'wrow', axis=2, tiled=True)  115 us
    unnamed x5, waiting for transfers between devices  109 us
    dot_general x4, matrix products, one_block(): jnp.einsum('pvh,gh->pvg', vale_sel, w_tile, preferred_element_type=jnp.fl...  41.1 us
    gather x4, local copies, waits for them, and re-layouts, one_block(): vale_sel = jnp.take(vale_flat, chosen, axis=0)  16.5 us
    unnamed x6, local copies, waits for them, and re-layouts  15.3 us
    gather x4, local copies, waits for them, and re-layouts, one_block(): cond_sel = jnp.take(cond_flat, chosen, axis=0)  7.18 us
  transfers between devices with their start and end apart: 4, of which 3 were waited for; matrix products, arithmetic and copies ran while one was open for 4% of the time, Pallas kernels for 0%

commit v1 on v0

v1 whole, which is shorter than its diff:
```python
import functools

import jax
import jax.numpy as jnp
from jax import lax
from jax.experimental import pallas as pl
from jax.experimental.pallas import tpu as pltpu
from jax.sharding import PartitionSpec as P


C = 8
V = 8
AXES = ("wrow", "kblk")
GROUP = 3
PIECES = 8


def pairs_of(n, m, move):
    return [(w * m + c, move(w, c) * m + c) for w in range(n) for c in range(m)]


def move(array, n, m, to):
    return lax.ppermute(array, AXES, pairs_of(n, m, to))


def gather_valence(own, n, m):
    to_a = lambda w, c: w ^ (1 if c % 2 == 0 else 2)
    to_b = lambda w, c: w ^ (2 if c % 2 == 0 else 1)
    near, far = (lambda w, c: w ^ 4), (lambda z: lambda w, c: w ^ (4 * z))
    base = [own]
    for z in range(1, n // 4):
        if z % 2 == 0:
            base.append(move(own, n, m, far(z)))
        else:
            base.append(move(base[z - 1], n, m, near))
    in_a, in_b, in_ab = [], [], []
    for z in range(n // 4):
        if z == 1:
            in_a.append(move(in_a[0], n, m, near))
            in_ab.append(move(in_ab[0], n, m, near))
        else:
            in_a.append(move(base[z], n, m, to_a))
            in_ab.append(move(in_a[z], n, m, to_b))
        in_b.append(move(base[z], n, m, to_b))
    return [slot for four in zip(base, in_a, in_b, in_ab) for slot in four]


def project_kernel(cap, kp, blocks, me, cond, w, *refs):
    x, lhs, slot = refs[-3:]
    q, t = pl.program_id(0), pl.program_id(1)
    pair_count, comps, _ = cond.shape
    width = w.shape[2]

    @pl.when(t == 0)
    def _():
        count = jnp.int32(0)
        for p in range(pair_count):
            match = blocks[p // kp, p % kp] == q

            @pl.when(match)
            def _():
                source = ((p // kp) ^ me[0]) * kp + p % kp
                lhs[count] = cond[source]
                slot[count] = p

            count = count + match.astype(jnp.int32)
        slot[cap] = count

    left = slot[cap]
    columns = pl.ds(pl.multiple_of(t * width, width), width)
    for first in range(0, cap, GROUP):
        for size in range(1, min(GROUP, cap - first) + 1):
            last = size == min(GROUP, cap - first)
            here = (left - first >= size) if last else (left - first == size)

            @pl.when(here)
            def _():
                rows = lhs[first : first + size].reshape(size * comps, lhs.shape[2])
                part = jnp.dot(rows, w[0], preferred_element_type=jnp.float32)
                for s in range(size):
                    x[slot[first + s], :, columns] = part[s * comps : (s + 1) * comps].astype(x.dtype)


def project(piece, pieces, kp, blocks, me, cond, screened):
    pair_count, comps, rows = cond.shape
    block_count, _, cols = screened.shape
    cap = 3 * pair_count // 8
    span = cols // pieces
    tile = min(1024, span)
    steps = span // tile
    return pl.pallas_call(
        functools.partial(project_kernel, cap, kp),
        out_shape=jax.ShapeDtypeStruct((pair_count, comps, span), cond.dtype),
        grid_spec=pltpu.PrefetchScalarGridSpec(
            num_scalar_prefetch=2,
            grid=(block_count, steps),
            in_specs=[
                pl.BlockSpec((pair_count, comps, rows), lambda q, t, *_: (0, 0, 0)),
                pl.BlockSpec((1, rows, tile), lambda q, t, *_: (q, 0, piece * steps + t)),
            ],
            out_specs=pl.BlockSpec((pair_count, comps, span), lambda q, t, *_: (0, 0, 0)),
            scratch_shapes=[
                pltpu.VMEM((cap, comps, rows), cond.dtype),
                pltpu.SMEM((cap + 1,), jnp.int32),
            ],
        ),
        compiler_params=pltpu.CompilerParams(vmem_limit_bytes=16 << 20),
        cost_estimate=pl.CostEstimate(
            flops=2 * pair_count * comps * rows * span,
            bytes_accessed=2 * (block_count * rows * span + pair_count * comps * (rows + span)),
            transcendentals=0,
        ),
        name="project",
    )(blocks, me, cond, screened)


def contract_kernel(kp, parts, n, row_of, col_of, *refs):
    xs, vale = refs[: -n - 1], refs[-n - 1 : -1]
    out = refs[-1]
    comps, width = xs[0].shape[1:]
    k_count = xs[0].shape[0] // kp
    rows = vale[0].shape[0] // k_count
    total = n * rows
    local = rows // kp
    index = lax.broadcasted_iota(jnp.int32, (total, total), 0)
    slot, inner = index // rows, index % rows
    swapped = (slot // 4) * 4 + (slot % 2) * 2 + (slot // 2) % 2
    comp = (jnp.where(col_of[0] % 2 == 0, slot, swapped) ^ row_of[0]) * local + inner % local
    lanes = total // parts
    size = lanes // kp
    target = (comp // size) * lanes + (inner // local) * size + comp % size
    order = (target == lax.broadcasted_iota(jnp.int32, (total, total), 1)).astype(jnp.float32)
    of_kp = (lax.broadcasted_iota(jnp.int32, (comps, total), 1) // local) % kp

    picked = []
    for k in range(k_count):
        acc = jnp.zeros((kp * comps, total), jnp.float32)
        for t, x in enumerate(xs):
            left = x[k * kp : (k + 1) * kp].reshape(kp * comps, width)
            right = jnp.concatenate([v[k * rows : (k + 1) * rows, t * width : (t + 1) * width] for v in vale], axis=0)
            acc += lax.dot_general(left, right, (((1,), (1,)), ((), ())), preferred_element_type=jnp.float32)
        one = jnp.zeros((comps, total), jnp.float32)
        for j in range(kp):
            one = jnp.where(of_kp == j, acc[j * comps : (j + 1) * comps], one)
        picked.append(one)
    ordered = jnp.dot(
        jnp.concatenate(picked, axis=0),
        order,
        precision=lax.Precision.HIGHEST,
        preferred_element_type=jnp.float32,
    )
    for k in range(k_count):
        for c in range(C):
            for part in range(parts):
                row = k * comps + c * C
                out[c * parts + part, k] = ordered[row : row + C, part * lanes : (part + 1) * lanes]


def contract(kp, k_count, parts, row, col, xs, slots):
    pair_count, comps, _ = xs[0].shape
    rows, cols = slots[0].shape
    n = len(slots)
    total = n * rows // k_count
    return pl.pallas_call(
        functools.partial(contract_kernel, kp, parts, n),
        out_shape=jax.ShapeDtypeStruct((C * parts, k_count, C, total // parts), jnp.float32),
        in_specs=[pl.BlockSpec(memory_space=pltpu.SMEM)] * 2 + [pl.BlockSpec(memory_space=pltpu.VMEM)] * (len(xs) + n),
        out_specs=pl.BlockSpec(memory_space=pltpu.VMEM),
        compiler_params=pltpu.CompilerParams(vmem_limit_bytes=32 << 20),
        cost_estimate=pl.CostEstimate(
            flops=2 * pair_count * comps * total * cols,
            bytes_accessed=2 * cols * (pair_count * comps + n * rows),
            transcendentals=0,
        ),
        name="contract",
    )(row, col, *xs, *slots)


def per_device(n, m, *args):
    return direct_kernel(n, m, *args)


def direct_kernel(n, m, conduction, valence, screened, pair_block):
    k_count, kp = pair_block.shape
    comps = conduction.shape[2]
    pair_count = k_count * kp
    local = valence.shape[2]
    cols = valence.shape[3]
    w = lax.axis_index("wrow").astype(jnp.int32)
    c = lax.axis_index("kblk").astype(jnp.int32)

    conds = [conduction]
    for i in range(1, m):
        conds.append(lax.ppermute(conduction, AXES, [(a * m + b, a * m + (b ^ i)) for a in range(n) for b in range(m)]))
    own = valence.reshape(pair_count * local, cols)
    cond = jnp.concatenate(conds, axis=0).reshape(pair_count, comps, conduction.shape[3])
    me = (c * (k_count // m)).reshape(1)

    slots = gather_valence(own, n, m)
    xs = []
    for piece in range(PIECES):
        xs.append(project(piece, PIECES, kp, pair_block, me, cond, screened))

    parts = n // C
    width = V * V // parts
    mine = contract(kp, k_count, parts, w.reshape(1), c.reshape(1), xs, slots)

    sent = mine.reshape(n * k_count, C, kp * width)
    got = lax.all_to_all(sent, AXES, 0, 0, tiled=True)
    total = got.reshape(n * m, k_count // m, C, kp, width // V, V).sum(0)
    return total.transpose(0, 3, 2, 1, 4).reshape(k_count // m, width // V, kp * C * V)


def solution(mesh):
    n, m = mesh.shape["wrow"], mesh.shape["kblk"]
    return jax.shard_map(
        functools.partial(per_device, n, m),
        mesh=mesh,
        in_specs=(
            P("kblk", None, None, "wrow"),
            P(None, None, "wrow", "kblk"),
            P(None, "wrow", "kblk"),
            P(),
        ),
        out_specs=P("kblk", "wrow", None),
        check_vma=False,
    )
```

time: 347 us -> 116 us (0.33)
  waiting for transfers between devices: 231 us -> 27.1 us
  Pallas kernels: 0 us -> 50 us
  matrix products: 48.4 us -> 0 us
  local copies, waits for them, and re-layouts: 49.3 us -> 3.48 us
  starting transfers between devices: 0.12 us -> 20.6 us
  between operations: 13.8 us -> 0.19 us
  blocking collectives: 0 us -> 12.8 us
    all_gather x2 -> x0, waiting for transfers between devices: 115 us -> none  [the longest x1 115 us: per_device(): gathered_vale = lax.all_gather(valence, 'wrow', axis=2, tiled=True)]
    unnamed x5 -> x0, waiting for transfers between devices: 109 us -> none
    pallas_call x0 -> x9, Pallas kernels: none -> 50 us  [the longest x8 45.6 us: project(): pl.pallas_call(functools.partial(project_kernel, cap, kp), out_shape=jax....]
    dot_general x12 -> x0, matrix products: 48.4 us -> none  [the longest x4 41.1 us: one_block(): jnp.einsum('pvh,gh->pvg', vale_sel, w_tile, preferred_element_type=jnp.fl...]
    ppermute x0 -> x16, waiting for transfers between devices: none -> 27.1 us  [the longest x15 27.1 us: move(): return lax.ppermute(array, AXES, pairs_of(n, m, to))]
    gather x12 -> x0, local copies, waits for them, and re-layouts: 26.3 us -> none  [the longest x4 16.5 us: one_block(): vale_sel = jnp.take(vale_flat, chosen, axis=0)]
    ppermute x0 -> x16, starting transfers between devices: none -> 20.6 us  [the longest x15 20.6 us: move(): return lax.ppermute(array, AXES, pairs_of(n, m, to))]
    unnamed x6 -> x8, local copies, waits for them, and re-layouts: 15.3 us -> 1.49 us
  transfers between devices with their start and end apart: 4 -> 16, of which waited for: 3 -> 2; matrix products, arithmetic and copies ran while one was open for 4% -> 1% of each run, Pallas kernels for 0% -> 39%
where the time goes in v1:
time: 116 us; the launch traced here: 115 us
  Pallas kernels  50 us (43%)
  waiting for transfers between devices  27.1 us (23%)
  starting transfers between devices  20.6 us (18%)
  blocking collectives  12.8 us (11%)
  local copies, waits for them, and re-layouts  3.48 us (3%)
  other arithmetic  1.33 us (1%)
    pallas_call x8, Pallas kernels, project(): pl.pallas_call(functools.partial(project_kernel, cap, kp), out_shape=jax....  45.6 us
    ppermute x15, waiting for transfers between devices, move(): return lax.ppermute(array, AXES, pairs_of(n, m, to))  27.1 us
    ppermute x15, starting transfers between devices, move(): return lax.ppermute(array, AXES, pairs_of(n, m, to))  20.6 us
    all_to_all x1, blocking collectives, direct_kernel(): got = lax.all_to_all(sent, AXES, 0, 0, tiled=True)  12.8 us
    pallas_call x1, Pallas kernels, contract(): pl.pallas_call(functools.partial(contract_kernel, kp, parts, n), out_shap...  4.42 us
  transfers between devices with their start and end apart: 16, of which 2 were waited for; matrix products, arithmetic and copies ran while one was open for 1% of the time, Pallas kernels for 39%

profile of v1, /device:TPU:0, one launch (start us, length us, event | category | flops | bytes accessed | tf_op | source)
XLA Modules:
  0.0 115.5 jit_solution(17959487553679491039)
XLA Ops:
  0.0 1.2 %reshape.26.refs_8_ = bf16[32,8192]{1,0:T(8,128)(2,1)S(1)} reshape(bf16[2,4,4,8192]{3,2,1,0:T(4,128)(2,1)} %param.5) | data formatting | bytes 1048576 | tf_op jit(solution)/shard_map/reshape | solution.py:195
  1.2 4.1 %collective-permute-start.8 = (bf16[32,8192]{1,0:T(8,128)(2,1)S(1)}, bf16[32,8192]{1,0:T(8,128)(2,1)S(1)}, u32[]{:S(2)}, u32[]{:S(2)}) collective-permute-start(bf16[32,8192]{1,0:T(8,128)(2,1)S(1)} %reshape.26.refs_8_), channel_id=1, source_target_pairs={{0,16},{1,17},{2,18},{3,19},{4,20},{5,21},{6,22},{7,23},{8,24},{9,... | collective-permute-start | bytes 1572872 | tf_op jit(solution)/shard_map/ppermute | solution.py:23
  5.3 1.5 %collective-permute-start.1 = (bf16[32,8192]{1,0:T(8,128)(2,1)S(1)}, bf16[32,8192]{1,0:T(8,128)(2,1)S(1)}, u32[]{:S(2)}, u32[]{:S(2)}) collective-permute-start(bf16[32,8192]{1,0:T(8,128)(2,1)S(1)} %reshape.26.refs_8_), channel_id=1, source_target_pairs={{0,2},{1,5},{2,0},{3,7},{4,6},{5,1},{6,4},{7,3},{8,10},{9,13},{10,... | collective-permute-start | bytes 1572872 | tf_op jit(solution)/shard_map/ppermute | solution.py:23
  6.8 1.6 %collective-permute-start.4 = (bf16[32,8192]{1,0:T(8,128)(2,1)S(1)}, bf16[32,8192]{1,0:T(8,128)(2,1)S(1)}, u32[]{:S(2)}, u32[]{:S(2)}) collective-permute-start(bf16[32,8192]{1,0:T(8,128)(2,1)S(1)} %reshape.26.refs_8_), channel_id=1, source_target_pairs={{0,8},{1,9},{2,10},{3,11},{4,12},{5,13},{6,14},{7,15},{8,0},{9,1},... | collective-permute-start | bytes 1572872 | tf_op jit(solution)/shard_map/ppermute | solution.py:23
  8.4 1.5 %collective-permute-start.2 = (bf16[32,8192]{1,0:T(8,128)(2,1)S(1)}, bf16[32,8192]{1,0:T(8,128)(2,1)S(1)}, u32[]{:S(2)}, u32[]{:S(2)}) collective-permute-start(bf16[32,8192]{1,0:T(8,128)(2,1)S(1)} %reshape.26.refs_8_), channel_id=1, source_target_pairs={{0,4},{1,3},{2,6},{3,1},{4,0},{5,7},{6,2},{7,5},{8,12},{9,11},{10,... | collective-permute-start | bytes 1572872 | tf_op jit(solution)/shard_map/ppermute | solution.py:23
  9.9 18.7 %collective-permute-done.8.refs_16_ = bf16[32,8192]{1,0:T(8,128)(2,1)S(1)} collective-permute-done((bf16[32,8192]{1,0:T(8,128)(2,1)S(1)}, bf16[32,8192]{1,0:T(8,128)(2,1)S(1)}, u32[]{:S(2)}, u32[]{:S(2)}) %collective-permute-start.8) | collective-permute-done | bytes 524320 | tf_op jit(solution)/shard_map/ppermute | solution.py:23
  29.2 1.5 %collective-permute-start.9 = (bf16[32,8192]{1,0:T(8,128)(2,1)S(1)}, bf16[32,8192]{1,0:T(8,128)(2,1)S(1)}, u32[]{:S(2)}, u32[]{:S(2)}) collective-permute-start(bf16[32,8192]{1,0:T(8,128)(2,1)S(1)} %collective-permute-done.8.refs_16_), channel_id=1, source_target_pairs={{0,2},{1,5},{2,0},{3,7},{4,6},{5,1},{6,4},{7,3},{8,10},{9,13},{10,... | collective-permute-start | bytes 1572872 | tf_op jit(solution)/shard_map/ppermute | solution.py:23
  30.7 1.5 %collective-permute-start.3 = (bf16[32,8192]{1,0:T(8,128)(2,1)S(1)}, bf16[32,8192]{1,0:T(8,128)(2,1)}, u32[]{:S(2)}, u32[]{:S(2)}) collective-permute-start(bf16[32,8192]{1,0:T(8,128)(2,1)S(1)} %collective-permute-done.1.refs_9_), channel_id=1, source_target_pairs={{0,4},{1,3},{2,6},{3,1},{4,0},{5,7},{6,2},{7,5},{8,12},{9,11},{10,... | collective-permute-start | bytes 1572872 | tf_op jit(solution)/shard_map/ppermute | solution.py:23
  33.6 1.4 %collective-permute-start.5 = (bf16[32,8192]{1,0:T(8,128)(2,1)S(1)}, bf16[32,8192]{1,0:T(8,128)(2,1)}, u32[]{:S(2)}, u32[]{:S(2)}) collective-permute-start(bf16[32,8192]{1,0:T(8,128)(2,1)S(1)} %collective-permute-done.1.refs_9_), channel_id=1, source_target_pairs={{0,8},{1,9},{2,10},{3,11},{4,12},{5,13},{6,14},{7,15},{8,0},{9,1},... | collective-permute-start | bytes 1572872 | tf_op jit(solution)/shard_map/ppermute | solution.py:23
  35.0 8.4 %collective-permute-done.12.refs_20_ = bf16[32,8192]{1,0:T(8,128)(2,1)S(1)} collective-permute-done((bf16[32,8192]{1,0:T(8,128)(2,1)S(1)}, bf16[32,8192]{1,0:T(8,128)(2,1)S(1)}, u32[]{:S(2)}, u32[]{:S(2)}) %collective-permute-start.12) | collective-permute-done | bytes 524320 | tf_op jit(solution)/shard_map/ppermute | solution.py:23
  43.4 1.5 %collective-permute-start.13 = (bf16[32,8192]{1,0:T(8,128)(2,1)S(1)}, bf16[32,8192]{1,0:T(8,128)(2,1)}, u32[]{:S(2)}, u32[]{:S(2)}) collective-permute-start(bf16[32,8192]{1,0:T(8,128)(2,1)S(1)} %collective-permute-done.12.refs_20_), channel_id=1, source_target_pairs={{0,2},{1,5},{2,0},{3,7},{4,6},{5,1},{6,4},{7,3},{8,10},{9,13},{10,... | collective-permute-start | bytes 1572872 | tf_op jit(solution)/shard_map/ppermute | solution.py:23
  44.9 1.3 %pad_maximum_fusion = bf16[2,4,64,1024]{3,2,1,0:T(8,128)(2,1)S(1)} fusion(bf16[1,4,64,1024]{3,2,1,0:T(8,128)(2,1)} %copy-done.3, bf16[1,4,64,1024]{3,2,1,0:T(8,128)(2,1)} %param.4), kind=kLoop, calls=%fused_computation | loop fusion | flops 524288 | bytes 2097152 | tf_op jit(solution)/shard_map/concatenate | solution.py:196
  46.9 5.7 %project.8.refs_0_ = bf16[8,64,1024]{2,1,0:T(8,128)(2,1)S(1)} custom-call(s32[2,4]{1,0:T(2,128)S(1)} %copy-done.2, s32[1]{0:T(128)} %bitcast.1.me.col_of, bf16[8,64,1024]{2,1,0:T(8,128)(2,1)S(1)} %bitcast.7, bf16[4,1024,8192]{2,1,0:T(8,128)(2,1)} %w.15), custom_call_target="tpu_custom_call" | custom-call | flops 1073741824 | bytes 10485760 | tf_op jit(solution)/shard_map/project/pallas_call | solution.py:91
  52.6 5.7 %project.9.refs_1_ = bf16[8,64,1024]{2,1,0:T(8,128)(2,1)S(1)} custom-call(s32[2,4]{1,0:T(2,128)S(1)} %copy-done.2, s32[1]{0:T(128)} %bitcast.1.me.col_of, bf16[8,64,1024]{2,1,0:T(8,128)(2,1)S(1)} %bitcast.8, bf16[4,1024,8192]{2,1,0:T(8,128)(2,1)} %w.15), custom_call_target="tpu_custom_call" | custom-call | flops 1073741824 | bytes 10485760 | tf_op jit(solution)/shard_map/project/pallas_call | solution.py:91
  58.3 1.6 %collective-permute-start.6 = (bf16[32,8192]{1,0:T(8,128)(2,1)S(1)}, bf16[32,8192]{1,0:T(8,128)(2,1)S(1)}, u32[]{:S(2)}, u32[]{:S(2)}) collective-permute-start(bf16[32,8192]{1,0:T(8,128)(2,1)S(1)} %collective-permute-done.4.refs_12_), channel_id=1, source_target_pairs={{0,4},{1,3},{2,6},{3,1},{4,0},{5,7},{6,2},{7,5},{8,12},{9,11},{10,... | collective-permute-start | bytes 1572872 | tf_op jit(solution)/shard_map/ppermute | solution.py:23
  60.4 1.5 %collective-permute-start.11 = (bf16[32,8192]{1,0:T(8,128)(2,1)S(1)}, bf16[32,8192]{1,0:T(8,128)(2,1)S(1)}, u32[]{:S(2)}, u32[]{:S(2)}) collective-permute-start(bf16[32,8192]{1,0:T(8,128)(2,1)S(1)} %collective-permute-done.9.refs_17_), channel_id=1, source_target_pairs={{0,4},{1,3},{2,6},{3,1},{4,0},{5,7},{6,2},{7,5},{8,12},{9,11},{10,... | collective-permute-start | bytes 1572872 | tf_op jit(solution)/shard_map/ppermute | solution.py:23
  63.0 5.7 %project.10.refs_2_ = bf16[8,64,1024]{2,1,0:T(8,128)(2,1)S(1)} custom-call(s32[2,4]{1,0:T(2,128)S(1)} %copy-done.2, s32[1]{0:T(128)} %bitcast.1.me.col_of, bf16[8,64,1024]{2,1,0:T(8,128)(2,1)S(1)} %bitcast.9, bf16[4,1024,8192]{2,1,0:T(8,128)(2,1)} %w.15), custom_call_target="tpu_custom_call" | custom-call | flops 1073741824 | bytes 10485760 | tf_op jit(solution)/shard_map/project/pallas_call | solution.py:91
  68.8 5.7 %project.11.refs_3_ = bf16[8,64,1024]{2,1,0:T(8,128)(2,1)S(1)} custom-call(s32[2,4]{1,0:T(2,128)S(1)} %copy-done.2, s32[1]{0:T(128)} %bitcast.1.me.col_of, bf16[8,64,1024]{2,1,0:T(8,128)(2,1)S(1)} %bitcast.10, bf16[4,1024,8192]{2,1,0:T(8,128)(2,1)} %w.15), custom_call_target="tpu_custom_call" | custom-call | flops 1073741824 | bytes 10485760 | tf_op jit(solution)/shard_map/project/pallas_call | solution.py:91
  74.5 5.7 %project.12.refs_4_ = bf16[8,64,1024]{2,1,0:T(8,128)(2,1)S(1)} custom-call(s32[2,4]{1,0:T(2,128)S(1)} %copy-done.2, s32[1]{0:T(128)} %bitcast.1.me.col_of, bf16[8,64,1024]{2,1,0:T(8,128)(2,1)S(1)} %bitcast.11, bf16[4,1024,8192]{2,1,0:T(8,128)(2,1)} %w.15), custom_call_target="tpu_custom_call" | custom-call | flops 1073741824 | bytes 10485760 | tf_op jit(solution)/shard_map/project/pallas_call | solution.py:91
  80.2 5.7 %project.13.refs_5_ = bf16[8,64,1024]{2,1,0:T(8,128)(2,1)S(1)} custom-call(s32[2,4]{1,0:T(2,128)S(1)} %copy-done.2, s32[1]{0:T(128)} %bitcast.1.me.col_of, bf16[8,64,1024]{2,1,0:T(8,128)(2,1)S(1)} %bitcast.12, bf16[4,1024,8192]{2,1,0:T(8,128)(2,1)} %w.15), custom_call_target="tpu_custom_call" | custom-call | flops 1073741824 | bytes 10485760 | tf_op jit(solution)/shard_map/project/pallas_call | solution.py:91
  85.9 5.7 %project.14.refs_6_ = bf16[8,64,1024]{2,1,0:T(8,128)(2,1)S(1)} custom-call(s32[2,4]{1,0:T(2,128)S(1)} %copy-done.2, s32[1]{0:T(128)} %bitcast.1.me.col_of, bf16[8,64,1024]{2,1,0:T(8,128)(2,1)S(1)} %bitcast.13, bf16[4,1024,8192]{2,1,0:T(8,128)(2,1)} %w.15), custom_call_target="tpu_custom_call" | custom-call | flops 1073741824 | bytes 10485760 | tf_op jit(solution)/shard_map/project/pallas_call | solution.py:91
  91.6 5.7 %project.15.refs_7_ = bf16[8,64,1024]{2,1,0:T(8,128)(2,1)S(1)} custom-call(s32[2,4]{1,0:T(2,128)S(1)} %copy-done.2, s32[1]{0:T(128)} %bitcast.1.me.col_of, bf16[8,64,1024]{2,1,0:T(8,128)(2,1)S(1)} %bitcast.14, bf16[4,1024,8192]{2,1,0:T(8,128)(2,1)} %w.15), custom_call_target="tpu_custom_call" | custom-call | flops 1073741824 | bytes 10485760 | tf_op jit(solution)/shard_map/project/pallas_call | solution.py:91
  97.4 4.4 %contract.1 = f32[16,2,8,128]{3,2,1,0:T(8,128)S(1)} custom-call(s32[1]{0:T(128)} %bitcast.row_of, s32[1]{0:T(128)} %bitcast.1.me.col_of, bf16[8,64,1024]{2,1,0:T(8,128)(2,1)S(1)} %project.8.refs_0_, bf16[8,64,1024]{2,1,0:T(8,128)(2,1)S(1)} %project.9.refs_1_, bf16[8,64,1024]{2,1,0:T(8,128)(2,1)S(1)} %project.10.refs_2_, ...), custom_call_target="tpu_custom_call" | custom-call | flops 2147483648 | bytes 16777216 | tf_op jit(solution)/shard_map/contract/pallas_call | solution.py:164
  101.8 12.8 %all_to_all.5 = f32[32,8,128]{2,1,0:T(8,128)S(1)} all-to-all(f32[32,8,128]{2,1,0:T(8,128)S(1)} %bitcast.15), channel_id=1, replica_groups=mesh['wrow'=16,'kblk'=2] {'wrow','kblk'}, dimensions={0} | all-to-all | bytes 262144 | tf_op jit(solution)/shard_map/all_to_all | solution.py:209
  (32 shorter events, 5.2 us)
Async XLA Ops:
  1.2 27.4 %collective-permute-start.8 = (bf16[32,8192]{1,0:T(8,128)(2,1)S(1)}, bf16[32,8192]{1,0:T(8,128)(2,1)S(1)}, u32[]{:S(2)}, u32[]{:S(2)}) collective-permute-start(bf16[32,8192]{1,0:T(8,128)(2,1)S(1)} %reshape.26.refs_8_), channel_id=1, source_target_pairs={{0,16},{1,17},{2,18},{3,19},{4,20},{5,21},{6,22},{7,23},{8,24},{9,... | collective-permute-start | bytes 1572872 | tf_op jit(solution)/shard_map/ppermute | solution.py:23
  5.3 23.9 %collective-permute-start = (bf16[1,4,64,1024]{3,2,1,0:T(8,128)(2,1)}, bf16[1,4,64,1024]{3,2,1,0:T(8,128)(2,1)S(1)}, u32[]{:S(2)}, u32[]{:S(2)}) collective-permute-start(bf16[1,4,64,1024]{3,2,1,0:T(8,128)(2,1)} %param.4), channel_id=1, source_target_pairs={{0,1},{1,0},{2,3},{3,2},{4,5},{5,4},{6,7},{7,6},{8,9},{9,8},{10,11... | collective-permute-start | bytes 1572872 | tf_op jit(solution)/shard_map/ppermute | solution.py:194
  5.3 25.4 %collective-permute-start.1 = (bf16[32,8192]{1,0:T(8,128)(2,1)S(1)}, bf16[32,8192]{1,0:T(8,128)(2,1)S(1)}, u32[]{:S(2)}, u32[]{:S(2)}) collective-permute-start(bf16[32,8192]{1,0:T(8,128)(2,1)S(1)} %reshape.26.refs_8_), channel_id=1, source_target_pairs={{0,2},{1,5},{2,0},{3,7},{4,6},{5,1},{6,4},{7,3},{8,10},{9,13},{10,... | collective-permute-start | bytes 1572872 | tf_op jit(solution)/shard_map/ppermute | solution.py:23
  6.8 25.5 %collective-permute-start.4 = (bf16[32,8192]{1,0:T(8,128)(2,1)S(1)}, bf16[32,8192]{1,0:T(8,128)(2,1)S(1)}, u32[]{:S(2)}, u32[]{:S(2)}) collective-permute-start(bf16[32,8192]{1,0:T(8,128)(2,1)S(1)} %reshape.26.refs_8_), channel_id=1, source_target_pairs={{0,8},{1,9},{2,10},{3,11},{4,12},{5,13},{6,14},{7,15},{8,0},{9,1},... | collective-permute-start | bytes 1572872 | tf_op jit(solution)/shard_map/ppermute | solution.py:23
  8.4 24.4 %collective-permute-start.2 = (bf16[32,8192]{1,0:T(8,128)(2,1)S(1)}, bf16[32,8192]{1,0:T(8,128)(2,1)S(1)}, u32[]{:S(2)}, u32[]{:S(2)}) collective-permute-start(bf16[32,8192]{1,0:T(8,128)(2,1)S(1)} %reshape.26.refs_8_), channel_id=1, source_target_pairs={{0,4},{1,3},{2,6},{3,1},{4,0},{5,7},{6,2},{7,5},{8,12},{9,11},{10,... | collective-permute-start | bytes 1572872 | tf_op jit(solution)/shard_map/ppermute | solution.py:23
  28.6 14.8 %collective-permute-start.12 = (bf16[32,8192]{1,0:T(8,128)(2,1)S(1)}, bf16[32,8192]{1,0:T(8,128)(2,1)S(1)}, u32[]{:S(2)}, u32[]{:S(2)}) collective-permute-start(bf16[32,8192]{1,0:T(8,128)(2,1)S(1)} %collective-permute-done.8.refs_16_), channel_id=1, source_target_pairs={{0,8},{1,9},{2,10},{3,11},{4,12},{5,13},{6,14},{7,15},{8,0},{9,1},... | collective-permute-start | bytes 1572872 | tf_op jit(solution)/shard_map/ppermute | solution.py:23
  29.2 14.1 %copy-start.3 = (bf16[1,4,64,1024]{3,2,1,0:T(8,128)(2,1)}, bf16[1,4,64,1024]{3,2,1,0:T(8,128)(2,1)S(1)}, u32[]{:S(2)}) copy-start(bf16[1,4,64,1024]{3,2,1,0:T(8,128)(2,1)S(1)} %collective-permute-done) | copy-start | bytes 1572868
  29.2 29.1 %collective-permute-start.9 = (bf16[32,8192]{1,0:T(8,128)(2,1)S(1)}, bf16[32,8192]{1,0:T(8,128)(2,1)S(1)}, u32[]{:S(2)}, u32[]{:S(2)}) collective-permute-start(bf16[32,8192]{1,0:T(8,128)(2,1)S(1)} %collective-permute-done.8.refs_16_), channel_id=1, source_target_pairs={{0,2},{1,5},{2,0},{3,7},{4,6},{5,1},{6,4},{7,3},{8,10},{9,13},{10,... | collective-permute-start | bytes 1572872 | tf_op jit(solution)/shard_map/ppermute | solution.py:23
  30.7 29.2 %collective-permute-start.3 = (bf16[32,8192]{1,0:T(8,128)(2,1)S(1)}, bf16[32,8192]{1,0:T(8,128)(2,1)}, u32[]{:S(2)}, u32[]{:S(2)}) collective-permute-start(bf16[32,8192]{1,0:T(8,128)(2,1)S(1)} %collective-permute-done.1.refs_9_), channel_id=1, source_target_pairs={{0,4},{1,3},{2,6},{3,1},{4,0},{5,7},{6,2},{7,5},{8,12},{9,11},{10,... | collective-permute-start | bytes 1572872 | tf_op jit(solution)/shard_map/ppermute | solution.py:23
  32.2 28.2 %collective-permute-start.10 = (bf16[32,8192]{1,0:T(8,128)(2,1)S(1)}, bf16[32,8192]{1,0:T(8,128)(2,1)}, u32[]{:S(2)}, u32[]{:S(2)}) collective-permute-start(bf16[32,8192]{1,0:T(8,128)(2,1)S(1)} %collective-permute-done.8.refs_16_), channel_id=1, source_target_pairs={{0,4},{1,3},{2,6},{3,1},{4,0},{5,7},{6,2},{7,5},{8,12},{9,11},{10,... | collective-permute-start | bytes 1572872 | tf_op jit(solution)/shard_map/ppermute | solution.py:23
  32.8 0.8 copy-start
  33.6 28.4 %collective-permute-start.5 = (bf16[32,8192]{1,0:T(8,128)(2,1)S(1)}, bf16[32,8192]{1,0:T(8,128)(2,1)}, u32[]{:S(2)}, u32[]{:S(2)}) collective-permute-start(bf16[32,8192]{1,0:T(8,128)(2,1)S(1)} %collective-permute-done.1.refs_9_), channel_id=1, source_target_pairs={{0,8},{1,9},{2,10},{3,11},{4,12},{5,13},{6,14},{7,15},{8,0},{9,1},... | collective-permute-start | bytes 1572872 | tf_op jit(solution)/shard_map/ppermute | solution.py:23
  43.4 19.2 %collective-permute-start.13 = (bf16[32,8192]{1,0:T(8,128)(2,1)S(1)}, bf16[32,8192]{1,0:T(8,128)(2,1)}, u32[]{:S(2)}, u32[]{:S(2)}) collective-permute-start(bf16[32,8192]{1,0:T(8,128)(2,1)S(1)} %collective-permute-done.12.refs_20_), channel_id=1, source_target_pairs={{0,2},{1,5},{2,0},{3,7},{4,6},{5,1},{6,4},{7,3},{8,10},{9,13},{10,... | collective-permute-start | bytes 1572872 | tf_op jit(solution)/shard_map/ppermute | solution.py:23
  46.2 0.7 copy-start.2
  58.3 39.0 %collective-permute-start.6 = (bf16[32,8192]{1,0:T(8,128)(2,1)S(1)}, bf16[32,8192]{1,0:T(8,128)(2,1)S(1)}, u32[]{:S(2)}, u32[]{:S(2)}) collective-permute-start(bf16[32,8192]{1,0:T(8,128)(2,1)S(1)} %collective-permute-done.4.refs_12_), channel_id=1, source_target_pairs={{0,4},{1,3},{2,6},{3,1},{4,0},{5,7},{6,2},{7,5},{8,12},{9,11},{10,... | collective-permute-start | bytes 1572872 | tf_op jit(solution)/shard_map/ppermute | solution.py:23
  59.9 37.4 %collective-permute-start.14 = (bf16[32,8192]{1,0:T(8,128)(2,1)S(1)}, bf16[32,8192]{1,0:T(8,128)(2,1)S(1)}, u32[]{:S(2)}, u32[]{:S(2)}) collective-permute-start(bf16[32,8192]{1,0:T(8,128)(2,1)S(1)} %collective-permute-done.12.refs_20_), channel_id=1, source_target_pairs={{0,4},{1,3},{2,6},{3,1},{4,0},{5,7},{6,2},{7,5},{8,12},{9,11},{10,... | collective-permute-start | bytes 1572872 | tf_op jit(solution)/shard_map/ppermute | solution.py:23
  60.4 36.9 %collective-permute-start.11 = (bf16[32,8192]{1,0:T(8,128)(2,1)S(1)}, bf16[32,8192]{1,0:T(8,128)(2,1)S(1)}, u32[]{:S(2)}, u32[]{:S(2)}) collective-permute-start(bf16[32,8192]{1,0:T(8,128)(2,1)S(1)} %collective-permute-done.9.refs_17_), channel_id=1, source_target_pairs={{0,4},{1,3},{2,6},{3,1},{4,0},{5,7},{6,2},{7,5},{8,12},{9,11},{10,... | collective-permute-start | bytes 1572872 | tf_op jit(solution)/shard_map/ppermute | solution.py:23
  61.9 35.4 %collective-permute-start.7 = (bf16[32,8192]{1,0:T(8,128)(2,1)}, bf16[32,8192]{1,0:T(8,128)(2,1)S(1)}, u32[]{:S(2)}, u32[]{:S(2)}) collective-permute-start(bf16[32,8192]{1,0:T(8,128)(2,1)} %collective-permute-done.3.refs_11_), channel_id=1, source_target_pairs={{0,8},{1,9},{2,10},{3,11},{4,12},{5,13},{6,14},{7,15},{8,0},{9,1},... | collective-permute-start | bytes 1572872 | tf_op jit(solution)/shard_map/ppermute | solution.py:23
  62.5 34.8 %collective-permute-start.15 = (bf16[32,8192]{1,0:T(8,128)(2,1)}, bf16[32,8192]{1,0:T(8,128)(2,1)S(1)}, u32[]{:S(2)}, u32[]{:S(2)}) collective-permute-start(bf16[32,8192]{1,0:T(8,128)(2,1)} %collective-permute-done.13.refs_21_), channel_id=1, source_target_pairs={{0,4},{1,3},{2,6},{3,1},{4,0},{5,7},{6,2},{7,5},{8,12},{9,11},{10,... | collective-permute-start | bytes 1572872 | tf_op jit(solution)/shard_map/ppermute | solution.py:23
  85.9 11.5 %copy-start.1 = (bf16[32,8192]{1,0:T(8,128)(2,1)S(1)}, bf16[32,8192]{1,0:T(8,128)(2,1)}, u32[]{:S(2)}) copy-start(bf16[32,8192]{1,0:T(8,128)(2,1)} %copy-done) | copy-start | bytes 1572868

commit v2 on v1

--- a/solution.py
+++ b/solution.py
@@ -12,15 +12,16 @@
 V = 8
 AXES = ("wrow", "kblk")
 GROUP = 3
-PIECES = 8
-
-
-def pairs_of(n, m, move):
-    return [(w * m + c, move(w, c) * m + c) for w in range(n) for c in range(m)]
-
-
-def move(array, n, m, to):
-    return lax.ppermute(array, AXES, pairs_of(n, m, to))
+PIECES = 4
+AHEAD = 4
+
+
+def pairs_of(n, m, to, across):
+    return [(w * m + c, to(w, c) * m + across(c)) for w in range(n) for c in range(m)]
+
+
+def move(array, n, m, to, across=lambda c: c):
+    return lax.ppermute(array, AXES, pairs_of(n, m, to, across))
 
 
 def gather_valence(own, n, m):
@@ -45,73 +46,88 @@
     return [slot for four in zip(base, in_a, in_b, in_ab) for slot in four]
 
 
-def project_kernel(cap, kp, blocks, me, cond, w, *refs):
-    x, lhs, slot = refs[-3:]
-    q, t = pl.program_id(0), pl.program_id(1)
+def project_kernel(cap, kp, piece, blocks, me, row_of, cond, w, x, lhs, slot, tiles, arrived):
     pair_count, comps, _ = cond.shape
-    width = w.shape[2]
-
-    @pl.when(t == 0)
-    def _():
+    block_count, _, span = tiles.shape
+    halves = arrived.shape[1]
+    width = span // halves
+
+    def fetch(q, half):
+        return pltpu.make_async_copy(
+            w.at[q, :, pl.ds(piece * span + half * width, width)],
+            tiles.at[q, :, pl.ds(half * width, width)],
+            arrived.at[q, half],
+        )
+
+    for i in range(AHEAD):
+        fetch(i // halves, i % halves).start()
+
+    @pl.loop(0, block_count)
+    def _(q):
         count = jnp.int32(0)
         for p in range(pair_count):
             match = blocks[p // kp, p % kp] == q
 
             @pl.when(match)
             def _():
-                source = ((p // kp) ^ me[0]) * kp + p % kp
-                lhs[count] = cond[source]
+                lhs[count] = cond[((p // kp) ^ me[0]) * kp + p % kp]
                 slot[count] = p
 
             count = count + match.astype(jnp.int32)
-        slot[cap] = count
-
-    left = slot[cap]
-    columns = pl.ds(pl.multiple_of(t * width, width), width)
-    for first in range(0, cap, GROUP):
-        for size in range(1, min(GROUP, cap - first) + 1):
-            last = size == min(GROUP, cap - first)
-            here = (left - first >= size) if last else (left - first == size)
-
-            @pl.when(here)
+        for half in range(halves):
+            columns = pl.ds(half * width, width)
+            fetch(q, half).wait()
+            later, part_of = (half + AHEAD) // halves, (half + AHEAD) % halves
+
+            @pl.when(q + later < block_count)
             def _():
-                rows = lhs[first : first + size].reshape(size * comps, lhs.shape[2])
-                part = jnp.dot(rows, w[0], preferred_element_type=jnp.float32)
-                for s in range(size):
-                    x[slot[first + s], :, columns] = part[s * comps : (s + 1) * comps].astype(x.dtype)
-
-
-def project(piece, pieces, kp, blocks, me, cond, screened):
+                fetch(q + later, part_of).start()
+
+            for first in range(0, cap, GROUP):
+                size = min(GROUP, cap - first)
+
+                @pl.when(count > first)
+                def _():
+                    rows = lhs[first : first + size].reshape(size * comps, lhs.shape[2])
+                    part = jnp.dot(rows, tiles[q, :, columns], preferred_element_type=jnp.float32).astype(x.dtype)
+                    for s in range(size):
+
+                        @pl.when(count > first + s)
+                        def _():
+                            x[slot[first + s], :, columns] = part[s * comps : (s + 1) * comps]
+
+
+def project(piece, pieces, kp, blocks, me, row_of, cond, screened):
     pair_count, comps, rows = cond.shape
     block_count, _, cols = screened.shape
     cap = 3 * pair_count // 8
     span = cols // pieces
-    tile = min(1024, span)
-    steps = span // tile
+    halves = 2
     return pl.pallas_call(
-        functools.partial(project_kernel, cap, kp),
+        functools.partial(project_kernel, cap, kp, piece),
         out_shape=jax.ShapeDtypeStruct((pair_count, comps, span), cond.dtype),
-        grid_spec=pltpu.PrefetchScalarGridSpec(
-            num_scalar_prefetch=2,
-            grid=(block_count, steps),
-            in_specs=[
-                pl.BlockSpec((pair_count, comps, rows), lambda q, t, *_: (0, 0, 0)),
-                pl.BlockSpec((1, rows, tile), lambda q, t, *_: (q, 0, piece * steps + t)),
-            ],
-            out_specs=pl.BlockSpec((pair_count, comps, span), lambda q, t, *_: (0, 0, 0)),
-            scratch_shapes=[
-                pltpu.VMEM((cap, comps, rows), cond.dtype),
-                pltpu.SMEM((cap + 1,), jnp.int32),
-            ],
-        ),
-        compiler_params=pltpu.CompilerParams(vmem_limit_bytes=16 << 20),
+        in_specs=[
+            pl.BlockSpec(memory_space=pltpu.SMEM),
+            pl.BlockSpec(memory_space=pltpu.SMEM),
+            pl.BlockSpec(memory_space=pltpu.SMEM),
+            pl.BlockSpec(memory_space=pltpu.VMEM),
+            pl.BlockSpec(memory_space=pl.ANY),
+        ],
+        out_specs=pl.BlockSpec(memory_space=pltpu.VMEM),
+        scratch_shapes=[
+            pltpu.VMEM((cap, comps, rows), cond.dtype),
+            pltpu.SMEM((cap,), jnp.int32),
+            pltpu.VMEM((block_count, rows, span), screened.dtype),
+            pltpu.SemaphoreType.DMA((block_count, halves)),
+        ],
+        compiler_params=pltpu.CompilerParams(vmem_limit_bytes=24 << 20),
         cost_estimate=pl.CostEstimate(
             flops=2 * pair_count * comps * rows * span,
             bytes_accessed=2 * (block_count * rows * span + pair_count * comps * (rows + span)),
             transcendentals=0,
         ),
         name="project",
-    )(blocks, me, cond, screened)
+    )(blocks, me, row_of, cond, screened)
 
 
 def contract_kernel(kp, parts, n, row_of, col_of, *refs):
@@ -166,7 +182,7 @@
         out_shape=jax.ShapeDtypeStruct((C * parts, k_count, C, total // parts), jnp.float32),
         in_specs=[pl.BlockSpec(memory_space=pltpu.SMEM)] * 2 + [pl.BlockSpec(memory_space=pltpu.VMEM)] * (len(xs) + n),
         out_specs=pl.BlockSpec(memory_space=pltpu.VMEM),
-        compiler_params=pltpu.CompilerParams(vmem_limit_bytes=32 << 20),
+        compiler_params=pltpu.CompilerParams(vmem_limit_bytes=14 << 20),
         cost_estimate=pl.CostEstimate(
             flops=2 * pair_count * comps * total * cols,
             bytes_accessed=2 * cols * (pair_count * comps + n * rows),
@@ -189,17 +205,17 @@
     w = lax.axis_index("wrow").astype(jnp.int32)
     c = lax.axis_index("kblk").astype(jnp.int32)
 
+    own = valence.reshape(pair_count * local, cols)
+    slots = gather_valence(own, n, m)
     conds = [conduction]
     for i in range(1, m):
-        conds.append(lax.ppermute(conduction, AXES, [(a * m + b, a * m + (b ^ i)) for a in range(n) for b in range(m)]))
-    own = valence.reshape(pair_count * local, cols)
+        conds.append(move(conduction, n, m, lambda w, c: w, lambda c: c ^ i))
     cond = jnp.concatenate(conds, axis=0).reshape(pair_count, comps, conduction.shape[3])
     me = (c * (k_count // m)).reshape(1)
 
-    slots = gather_valence(own, n, m)
     xs = []
     for piece in range(PIECES):
-        xs.append(project(piece, PIECES, kp, pair_block, me, cond, screened))
+        xs.append(project(piece, PIECES, kp, pair_block, me, w.reshape(1), cond, screened))
 
     parts = n // C
     width = V * V // parts

time: 116 us -> 99.7 us (0.86)
  Pallas kernels: 50 us -> 34.7 us
  local copies, waits for them, and re-layouts: 3.48 us -> 2.01 us
    pallas_call x8 -> x4, Pallas kernels: 45.6 us -> 30.1 us  [project(): pl.pallas_call(functools.partial(project_kernel, cap, kp, piece), out_sha...]
    unnamed x8 -> x4, local copies, waits for them, and re-layouts: 1.49 us -> 0.01 us
  transfers between devices with their start and end apart: 16 -> 16, of which waited for: 2 -> 2; matrix products, arithmetic and copies ran while one was open for 1% -> 1% of each run, Pallas kernels for 39% -> 30%
where the time goes in v2:
time: 99.7 us; the launch traced here: 99.5 us
  Pallas kernels  34.7 us (35%)
  waiting for transfers between devices  27.9 us (28%)
  starting transfers between devices  20.6 us (21%)
  blocking collectives  12.8 us (13%)
  local copies, waits for them, and re-layouts  2.01 us (2%)
  other arithmetic  1.33 us (1%)
    pallas_call x4, Pallas kernels, project(): pl.pallas_call(functools.partial(project_kernel, cap, kp, piece), out_sha...  30.1 us
    ppermute x16, waiting for transfers between devices, move(): return lax.ppermute(array, AXES, pairs_of(n, m, to, across))  27.9 us
    ppermute x16, starting transfers between devices, move(): return lax.ppermute(array, AXES, pairs_of(n, m, to, across))  20.6 us
    all_to_all x1, blocking collectives, direct_kernel(): got = lax.all_to_all(sent, AXES, 0, 0, tiled=True)  12.8 us
    pallas_call x1, Pallas kernels, contract(): pl.pallas_call(functools.partial(contract_kernel, kp, parts, n), out_shap...  4.59 us
  transfers between devices with their start and end apart: 16, of which 2 were waited for; matrix products, arithmetic and copies ran while one was open for 1% of the time, Pallas kernels for 30%

profile of v2, /device:TPU:0, one launch (start us, length us, event | category | flops | bytes accessed | tf_op | source)
XLA Modules:
  0.0 99.5 jit_solution(4257965470674515718)
XLA Ops:
  0.0 1.2 %reshape.30.refs_4_ = bf16[32,8192]{1,0:T(8,128)(2,1)S(1)} reshape(bf16[2,4,4,8192]{3,2,1,0:T(4,128)(2,1)} %param.5) | data formatting | bytes 1048576 | tf_op jit(solution)/shard_map/reshape | solution.py:208
  1.2 4.1 %collective-permute-start.8 = (bf16[32,8192]{1,0:T(8,128)(2,1)S(1)}, bf16[32,8192]{1,0:T(8,128)(2,1)S(1)}, u32[]{:S(2)}, u32[]{:S(2)}) collective-permute-start(bf16[32,8192]{1,0:T(8,128)(2,1)S(1)} %reshape.30.refs_4_), channel_id=1, source_target_pairs={{0,16},{1,17},{2,18},{3,19},{4,20},{5,21},{6,22},{7,23},{8,24},{9,... | collective-permute-start | bytes 1572872 | tf_op jit(solution)/shard_map/ppermute | solution.py:24
  5.3 1.5 %collective-permute-start.1 = (bf16[32,8192]{1,0:T(8,128)(2,1)S(1)}, bf16[32,8192]{1,0:T(8,128)(2,1)S(1)}, u32[]{:S(2)}, u32[]{:S(2)}) collective-permute-start(bf16[32,8192]{1,0:T(8,128)(2,1)S(1)} %reshape.30.refs_4_), channel_id=1, source_target_pairs={{0,2},{1,5},{2,0},{3,7},{4,6},{5,1},{6,4},{7,3},{8,10},{9,13},{10,... | collective-permute-start | bytes 1572872 | tf_op jit(solution)/shard_map/ppermute | solution.py:24
  6.8 1.6 %collective-permute-start.4 = (bf16[32,8192]{1,0:T(8,128)(2,1)S(1)}, bf16[32,8192]{1,0:T(8,128)(2,1)S(1)}, u32[]{:S(2)}, u32[]{:S(2)}) collective-permute-start(bf16[32,8192]{1,0:T(8,128)(2,1)S(1)} %reshape.30.refs_4_), channel_id=1, source_target_pairs={{0,8},{1,9},{2,10},{3,11},{4,12},{5,13},{6,14},{7,15},{8,0},{9,1},... | collective-permute-start | bytes 1572872 | tf_op jit(solution)/shard_map/ppermute | solution.py:24
  8.4 1.5 %collective-permute-start.2 = (bf16[32,8192]{1,0:T(8,128)(2,1)S(1)}, bf16[32,8192]{1,0:T(8,128)(2,1)S(1)}, u32[]{:S(2)}, u32[]{:S(2)}) collective-permute-start(bf16[32,8192]{1,0:T(8,128)(2,1)S(1)} %reshape.30.refs_4_), channel_id=1, source_target_pairs={{0,4},{1,3},{2,6},{3,1},{4,0},{5,7},{6,2},{7,5},{8,12},{9,11},{10,... | collective-permute-start | bytes 1572872 | tf_op jit(solution)/shard_map/ppermute | solution.py:24
  9.9 18.7 %collective-permute-done.8.refs_12_ = bf16[32,8192]{1,0:T(8,128)(2,1)S(1)} collective-permute-done((bf16[32,8192]{1,0:T(8,128)(2,1)S(1)}, bf16[32,8192]{1,0:T(8,128)(2,1)S(1)}, u32[]{:S(2)}, u32[]{:S(2)}) %collective-permute-start.8) | collective-permute-done | bytes 524320 | tf_op jit(solution)/shard_map/ppermute | solution.py:24
  28.6 0.7 collective-permute-start.12
  29.2 1.5 %collective-permute-start.9 = (bf16[32,8192]{1,0:T(8,128)(2,1)S(1)}, bf16[32,8192]{1,0:T(8,128)(2,1)}, u32[]{:S(2)}, u32[]{:S(2)}) collective-permute-start(bf16[32,8192]{1,0:T(8,128)(2,1)S(1)} %collective-permute-done.8.refs_12_), channel_id=1, source_target_pairs={{0,2},{1,5},{2,0},{3,7},{4,6},{5,1},{6,4},{7,3},{8,10},{9,13},{10,... | collective-permute-start | bytes 1572872 | tf_op jit(solution)/shard_map/ppermute | solution.py:24
  30.7 1.5 %collective-permute-start.3 = (bf16[32,8192]{1,0:T(8,128)(2,1)S(1)}, bf16[32,8192]{1,0:T(8,128)(2,1)}, u32[]{:S(2)}, u32[]{:S(2)}) collective-permute-start(bf16[32,8192]{1,0:T(8,128)(2,1)S(1)} %collective-permute-done.1.refs_5_), channel_id=1, source_target_pairs={{0,4},{1,3},{2,6},{3,1},{4,0},{5,7},{6,2},{7,5},{8,12},{9,11},{10,... | collective-permute-start | bytes 1572872 | tf_op jit(solution)/shard_map/ppermute | solution.py:24
  32.8 1.4 %collective-permute-start.5 = (bf16[32,8192]{1,0:T(8,128)(2,1)S(1)}, bf16[32,8192]{1,0:T(8,128)(2,1)}, u32[]{:S(2)}, u32[]{:S(2)}) collective-permute-start(bf16[32,8192]{1,0:T(8,128)(2,1)S(1)} %collective-permute-done.1.refs_5_), channel_id=1, source_target_pairs={{0,8},{1,9},{2,10},{3,11},{4,12},{5,13},{6,14},{7,15},{8,0},{9,1},... | collective-permute-start | bytes 1572872 | tf_op jit(solution)/shard_map/ppermute | solution.py:24
  34.2 9.2 %collective-permute-done.12.refs_16_ = bf16[32,8192]{1,0:T(8,128)(2,1)S(1)} collective-permute-done((bf16[32,8192]{1,0:T(8,128)(2,1)S(1)}, bf16[32,8192]{1,0:T(8,128)(2,1)S(1)}, u32[]{:S(2)}, u32[]{:S(2)}) %collective-permute-start.12) | collective-permute-done | bytes 524320 | tf_op jit(solution)/shard_map/ppermute | solution.py:24
  43.4 1.5 %collective-permute-start.13 = (bf16[32,8192]{1,0:T(8,128)(2,1)S(1)}, bf16[32,8192]{1,0:T(8,128)(2,1)}, u32[]{:S(2)}, u32[]{:S(2)}) collective-permute-start(bf16[32,8192]{1,0:T(8,128)(2,1)S(1)} %collective-permute-done.12.refs_16_), channel_id=1, source_target_pairs={{0,2},{1,5},{2,0},{3,7},{4,6},{5,1},{6,4},{7,3},{8,10},{9,13},{10,... | collective-permute-start | bytes 1572872 | tf_op jit(solution)/shard_map/ppermute | solution.py:24
  44.9 1.3 %pad_maximum_fusion = bf16[2,4,64,1024]{3,2,1,0:T(8,128)(2,1)S(1)} fusion(bf16[1,4,64,1024]{3,2,1,0:T(8,128)(2,1)} %copy-done.1, bf16[1,4,64,1024]{3,2,1,0:T(8,128)(2,1)} %param.4), kind=kLoop, calls=%fused_computation | loop fusion | flops 524288 | bytes 2097152 | tf_op jit(solution)/shard_map/concatenate | solution.py:213
  46.2 7.5 %project.5.refs_1_ = bf16[8,64,2048]{2,1,0:T(8,128)(2,1)S(1)} custom-call(s32[2,4]{1,0:T(2,128)S(1)} %copy-done, s32[1]{0:T(128)} %bitcast.1.me.col_of, s32[1]{0:T(128)} %bitcast.row_of, bf16[8,64,1024]{2,1,0:T(8,128)(2,1)S(1)} %bitcast.7, bf16[4,1024,8192]{2,1,0:T(8,128)(2,1)} %w.7), custom_call_target="tpu_custom_call" | custom-call | flops 2147483648 | bytes 19922944 | tf_op jit(solution)/shard_map/project/pallas_call | solution.py:106
  53.8 1.6 %collective-permute-start.6 = (bf16[32,8192]{1,0:T(8,128)(2,1)S(1)}, bf16[32,8192]{1,0:T(8,128)(2,1)S(1)}, u32[]{:S(2)}, u32[]{:S(2)}) collective-permute-start(bf16[32,8192]{1,0:T(8,128)(2,1)S(1)} %collective-permute-done.4.refs_8_), channel_id=1, source_target_pairs={{0,4},{1,3},{2,6},{3,1},{4,0},{5,7},{6,2},{7,5},{8,12},{9,11},{10,... | collective-permute-start | bytes 1572872 | tf_op jit(solution)/shard_map/ppermute | solution.py:24
  55.9 1.5 %collective-permute-start.11 = (bf16[32,8192]{1,0:T(8,128)(2,1)}, bf16[32,8192]{1,0:T(8,128)(2,1)S(1)}, u32[]{:S(2)}, u32[]{:S(2)}) collective-permute-start(bf16[32,8192]{1,0:T(8,128)(2,1)} %collective-permute-done.9.refs_13_), channel_id=1, source_target_pairs={{0,4},{1,3},{2,6},{3,1},{4,0},{5,7},{6,2},{7,5},{8,12},{9,11},{10,... | collective-permute-start | bytes 1572872 | tf_op jit(solution)/shard_map/ppermute | solution.py:24
  57.4 0.6 collective-permute-start.7
  58.0 0.5 collective-permute-start.15
  58.5 7.5 %project.6.refs_2_ = bf16[8,64,2048]{2,1,0:T(8,128)(2,1)S(1)} custom-call(s32[2,4]{1,0:T(2,128)S(1)} %copy-done, s32[1]{0:T(128)} %bitcast.1.me.col_of, s32[1]{0:T(128)} %bitcast.row_of, bf16[8,64,1024]{2,1,0:T(8,128)(2,1)S(1)} %bitcast.8, bf16[4,1024,8192]{2,1,0:T(8,128)(2,1)} %w.7), custom_call_target="tpu_custom_call" | custom-call | flops 2147483648 | bytes 19922944 | tf_op jit(solution)/shard_map/project/pallas_call | solution.py:106
  66.1 7.5 %project.7.refs_3_ = bf16[8,64,2048]{2,1,0:T(8,128)(2,1)S(1)} custom-call(s32[2,4]{1,0:T(2,128)S(1)} %copy-done, s32[1]{0:T(128)} %bitcast.1.me.col_of, s32[1]{0:T(128)} %bitcast.row_of, bf16[8,64,1024]{2,1,0:T(8,128)(2,1)S(1)} %bitcast.9, bf16[4,1024,8192]{2,1,0:T(8,128)(2,1)} %w.7), custom_call_target="tpu_custom_call" | custom-call | flops 2147483648 | bytes 19922944 | tf_op jit(solution)/shard_map/project/pallas_call | solution.py:106
  73.6 7.5 %project.4.refs_0_ = bf16[8,64,2048]{2,1,0:T(8,128)(2,1)S(1)} custom-call(s32[2,4]{1,0:T(2,128)S(1)} %copy-done, s32[1]{0:T(128)} %bitcast.1.me.col_of, s32[1]{0:T(128)} %bitcast.row_of, bf16[8,64,1024]{2,1,0:T(8,128)(2,1)S(1)} %bitcast.10, bf16[4,1024,8192]{2,1,0:T(8,128)(2,1)} %w.7), custom_call_target="tpu_custom_call" | custom-call | flops 2147483648 | bytes 19922944 | tf_op jit(solution)/shard_map/project/pallas_call | solution.py:106
  81.2 4.6 %contract.1 = f32[16,2,8,128]{3,2,1,0:T(8,128)S(1)} custom-call(s32[1]{0:T(128)} %bitcast.row_of, s32[1]{0:T(128)} %bitcast.1.me.col_of, bf16[8,64,2048]{2,1,0:T(8,128)(2,1)S(1)} %project.4.refs_0_, bf16[8,64,2048]{2,1,0:T(8,128)(2,1)S(1)} %project.5.refs_1_, bf16[8,64,2048]{2,1,0:T(8,128)(2,1)S(1)} %project.6.refs_2_, ...), custom_call_target="tpu_custom_call" | custom-call | flops 2147483648 | bytes 16777216 | tf_op jit(solution)/shard_map/contract/pallas_call | solution.py:180
  85.8 12.8 %all_to_all.5 = f32[32,8,128]{2,1,0:T(8,128)S(1)} all-to-all(f32[32,8,128]{2,1,0:T(8,128)S(1)} %bitcast.11), channel_id=1, replica_groups=mesh['wrow'=16,'kblk'=2] {'wrow','kblk'}, dimensions={0} | all-to-all | bytes 262144 | tf_op jit(solution)/shard_map/all_to_all | solution.py:225
  98.8 0.7 reshape.32
  (24 shorter events, 1.2 us)
Async XLA Ops:
  0.0 46.2 %copy-start = (s32[2,4]{1,0:T(2,128)S(1)}, s32[2,4]{1,0:T(2,128)}, u32[]{:S(2)}) copy-start(s32[2,4]{1,0:T(2,128)} %blocks.7) | copy-start | bytes 100
  1.2 27.4 %collective-permute-start.8 = (bf16[32,8192]{1,0:T(8,128)(2,1)S(1)}, bf16[32,8192]{1,0:T(8,128)(2,1)S(1)}, u32[]{:S(2)}, u32[]{:S(2)}) collective-permute-start(bf16[32,8192]{1,0:T(8,128)(2,1)S(1)} %reshape.30.refs_4_), channel_id=1, source_target_pairs={{0,16},{1,17},{2,18},{3,19},{4,20},{5,21},{6,22},{7,23},{8,24},{9,... | collective-permute-start | bytes 1572872 | tf_op jit(solution)/shard_map/ppermute | solution.py:24
  5.3 23.9 %collective-permute-start = (bf16[1,4,64,1024]{3,2,1,0:T(8,128)(2,1)}, bf16[1,4,64,1024]{3,2,1,0:T(8,128)(2,1)S(1)}, u32[]{:S(2)}, u32[]{:S(2)}) collective-permute-start(bf16[1,4,64,1024]{3,2,1,0:T(8,128)(2,1)} %param.4), channel_id=1, source_target_pairs={{0,1},{1,0},{2,3},{3,2},{4,5},{5,4},{6,7},{7,6},{8,9},{9,8},{10,11... | collective-permute-start | bytes 1572872 | tf_op jit(solution)/shard_map/ppermute | solution.py:24
  5.3 25.4 %collective-permute-start.1 = (bf16[32,8192]{1,0:T(8,128)(2,1)S(1)}, bf16[32,8192]{1,0:T(8,128)(2,1)S(1)}, u32[]{:S(2)}, u32[]{:S(2)}) collective-permute-start(bf16[32,8192]{1,0:T(8,128)(2,1)S(1)} %reshape.30.refs_4_), channel_id=1, source_target_pairs={{0,2},{1,5},{2,0},{3,7},{4,6},{5,1},{6,4},{7,3},{8,10},{9,13},{10,... | collective-permute-start | bytes 1572872 | tf_op jit(solution)/shard_map/ppermute | solution.py:24
  6.8 25.5 %collective-permute-start.4 = (bf16[32,8192]{1,0:T(8,128)(2,1)S(1)}, bf16[32,8192]{1,0:T(8,128)(2,1)S(1)}, u32[]{:S(2)}, u32[]{:S(2)}) collective-permute-start(bf16[32,8192]{1,0:T(8,128)(2,1)S(1)} %reshape.30.refs_4_), channel_id=1, source_target_pairs={{0,8},{1,9},{2,10},{3,11},{4,12},{5,13},{6,14},{7,15},{8,0},{9,1},... | collective-permute-start | bytes 1572872 | tf_op jit(solution)/shard_map/ppermute | solution.py:24
  8.4 24.4 %collective-permute-start.2 = (bf16[32,8192]{1,0:T(8,128)(2,1)S(1)}, bf16[32,8192]{1,0:T(8,128)(2,1)S(1)}, u32[]{:S(2)}, u32[]{:S(2)}) collective-permute-start(bf16[32,8192]{1,0:T(8,128)(2,1)S(1)} %reshape.30.refs_4_), channel_id=1, source_target_pairs={{0,4},{1,3},{2,6},{3,1},{4,0},{5,7},{6,2},{7,5},{8,12},{9,11},{10,... | collective-permute-start | bytes 1572872 | tf_op jit(solution)/shard_map/ppermute | solution.py:24
  28.6 14.8 %collective-permute-start.12 = (bf16[32,8192]{1,0:T(8,128)(2,1)S(1)}, bf16[32,8192]{1,0:T(8,128)(2,1)S(1)}, u32[]{:S(2)}, u32[]{:S(2)}) collective-permute-start(bf16[32,8192]{1,0:T(8,128)(2,1)S(1)} %collective-permute-done.8.refs_12_), channel_id=1, source_target_pairs={{0,8},{1,9},{2,10},{3,11},{4,12},{5,13},{6,14},{7,15},{8,0},{9,1},... | collective-permute-start | bytes 1572872 | tf_op jit(solution)/shard_map/ppermute | solution.py:24
  29.2 14.1 %copy-start.1 = (bf16[1,4,64,1024]{3,2,1,0:T(8,128)(2,1)}, bf16[1,4,64,1024]{3,2,1,0:T(8,128)(2,1)S(1)}, u32[]{:S(2)}) copy-start(bf16[1,4,64,1024]{3,2,1,0:T(8,128)(2,1)S(1)} %collective-permute-done) | copy-start | bytes 1572868
  29.2 24.5 %collective-permute-start.9 = (bf16[32,8192]{1,0:T(8,128)(2,1)S(1)}, bf16[32,8192]{1,0:T(8,128)(2,1)}, u32[]{:S(2)}, u32[]{:S(2)}) collective-permute-start(bf16[32,8192]{1,0:T(8,128)(2,1)S(1)} %collective-permute-done.8.refs_12_), channel_id=1, source_target_pairs={{0,2},{1,5},{2,0},{3,7},{4,6},{5,1},{6,4},{7,3},{8,10},{9,13},{10,... | collective-permute-start | bytes 1572872 | tf_op jit(solution)/shard_map/ppermute | solution.py:24
  30.7 24.6 %collective-permute-start.3 = (bf16[32,8192]{1,0:T(8,128)(2,1)S(1)}, bf16[32,8192]{1,0:T(8,128)(2,1)}, u32[]{:S(2)}, u32[]{:S(2)}) collective-permute-start(bf16[32,8192]{1,0:T(8,128)(2,1)S(1)} %collective-permute-done.1.refs_5_), channel_id=1, source_target_pairs={{0,4},{1,3},{2,6},{3,1},{4,0},{5,7},{6,2},{7,5},{8,12},{9,11},{10,... | collective-permute-start | bytes 1572872 | tf_op jit(solution)/shard_map/ppermute | solution.py:24
  32.3 23.6 %collective-permute-start.10 = (bf16[32,8192]{1,0:T(8,128)(2,1)S(1)}, bf16[32,8192]{1,0:T(8,128)(2,1)}, u32[]{:S(2)}, u32[]{:S(2)}) collective-permute-start(bf16[32,8192]{1,0:T(8,128)(2,1)S(1)} %collective-permute-done.8.refs_12_), channel_id=1, source_target_pairs={{0,4},{1,3},{2,6},{3,1},{4,0},{5,7},{6,2},{7,5},{8,12},{9,11},{10,... | collective-permute-start | bytes 1572872 | tf_op jit(solution)/shard_map/ppermute | solution.py:24
  32.8 24.6 %collective-permute-start.5 = (bf16[32,8192]{1,0:T(8,128)(2,1)S(1)}, bf16[32,8192]{1,0:T(8,128)(2,1)}, u32[]{:S(2)}, u32[]{:S(2)}) collective-permute-start(bf16[32,8192]{1,0:T(8,128)(2,1)S(1)} %collective-permute-done.1.refs_5_), channel_id=1, source_target_pairs={{0,8},{1,9},{2,10},{3,11},{4,12},{5,13},{6,14},{7,15},{8,0},{9,1},... | collective-permute-start | bytes 1572872 | tf_op jit(solution)/shard_map/ppermute | solution.py:24
  43.4 14.6 %collective-permute-start.13 = (bf16[32,8192]{1,0:T(8,128)(2,1)S(1)}, bf16[32,8192]{1,0:T(8,128)(2,1)}, u32[]{:S(2)}, u32[]{:S(2)}) collective-permute-start(bf16[32,8192]{1,0:T(8,128)(2,1)S(1)} %collective-permute-done.12.refs_16_), channel_id=1, source_target_pairs={{0,2},{1,5},{2,0},{3,7},{4,6},{5,1},{6,4},{7,3},{8,10},{9,13},{10,... | collective-permute-start | bytes 1572872 | tf_op jit(solution)/shard_map/ppermute | solution.py:24
  53.8 27.4 %collective-permute-start.6 = (bf16[32,8192]{1,0:T(8,128)(2,1)S(1)}, bf16[32,8192]{1,0:T(8,128)(2,1)S(1)}, u32[]{:S(2)}, u32[]{:S(2)}) collective-permute-start(bf16[32,8192]{1,0:T(8,128)(2,1)S(1)} %collective-permute-done.4.refs_8_), channel_id=1, source_target_pairs={{0,4},{1,3},{2,6},{3,1},{4,0},{5,7},{6,2},{7,5},{8,12},{9,11},{10,... | collective-permute-start | bytes 1572872 | tf_op jit(solution)/shard_map/ppermute | solution.py:24
  55.4 25.8 %collective-permute-start.14 = (bf16[32,8192]{1,0:T(8,128)(2,1)S(1)}, bf16[32,8192]{1,0:T(8,128)(2,1)S(1)}, u32[]{:S(2)}, u32[]{:S(2)}) collective-permute-start(bf16[32,8192]{1,0:T(8,128)(2,1)S(1)} %collective-permute-done.12.refs_16_), channel_id=1, source_target_pairs={{0,4},{1,3},{2,6},{3,1},{4,0},{5,7},{6,2},{7,5},{8,12},{9,11},{10,... | collective-permute-start | bytes 1572872 | tf_op jit(solution)/shard_map/ppermute | solution.py:24
  55.9 25.3 %collective-permute-start.11 = (bf16[32,8192]{1,0:T(8,128)(2,1)}, bf16[32,8192]{1,0:T(8,128)(2,1)S(1)}, u32[]{:S(2)}, u32[]{:S(2)}) collective-permute-start(bf16[32,8192]{1,0:T(8,128)(2,1)} %collective-permute-done.9.refs_13_), channel_id=1, source_target_pairs={{0,4},{1,3},{2,6},{3,1},{4,0},{5,7},{6,2},{7,5},{8,12},{9,11},{10,... | collective-permute-start | bytes 1572872 | tf_op jit(solution)/shard_map/ppermute | solution.py:24
  57.4 23.8 %collective-permute-start.7 = (bf16[32,8192]{1,0:T(8,128)(2,1)}, bf16[32,8192]{1,0:T(8,128)(2,1)S(1)}, u32[]{:S(2)}, u32[]{:S(2)}) collective-permute-start(bf16[32,8192]{1,0:T(8,128)(2,1)} %collective-permute-done.3.refs_7_), channel_id=1, source_target_pairs={{0,8},{1,9},{2,10},{3,11},{4,12},{5,13},{6,14},{7,15},{8,0},{9,1},... | collective-permute-start | bytes 1572872 | tf_op jit(solution)/shard_map/ppermute | solution.py:24
  58.0 23.2 %collective-permute-start.15 = (bf16[32,8192]{1,0:T(8,128)(2,1)}, bf16[32,8192]{1,0:T(8,128)(2,1)S(1)}, u32[]{:S(2)}, u32[]{:S(2)}) collective-permute-start(bf16[32,8192]{1,0:T(8,128)(2,1)} %collective-permute-done.13.refs_17_), channel_id=1, source_target_pairs={{0,4},{1,3},{2,6},{3,1},{4,0},{5,7},{6,2},{7,5},{8,12},{9,11},{10,... | collective-permute-start | bytes 1572872 | tf_op jit(solution)/shard_map/ppermute | solution.py:24

commit v3 on v2

--- a/solution.py
+++ b/solution.py
@@ -12,7 +12,7 @@
 V = 8
 AXES = ("wrow", "kblk")
 GROUP = 3
-PIECES = 4
+SPANS = (3, 1, 2, 2)
 AHEAD = 4
 
 
@@ -46,7 +46,7 @@
     return [slot for four in zip(base, in_a, in_b, in_ab) for slot in four]
 
 
-def project_kernel(cap, kp, piece, blocks, me, row_of, cond, w, x, lhs, slot, tiles, arrived):
+def project_kernel(cap, kp, start, blocks, me, row_of, cond, w, x, lhs, slot, tiles, arrived):
     pair_count, comps, _ = cond.shape
     block_count, _, span = tiles.shape
     halves = arrived.shape[1]
@@ -54,12 +54,12 @@
 
     def fetch(q, half):
         return pltpu.make_async_copy(
-            w.at[q, :, pl.ds(piece * span + half * width, width)],
+            w.at[q, :, pl.ds(start + half * width, width)],
             tiles.at[q, :, pl.ds(half * width, width)],
             arrived.at[q, half],
         )
 
-    for i in range(AHEAD):
+    for i in range(min(AHEAD, block_count * halves)):
         fetch(i // halves, i % halves).start()
 
     @pl.loop(0, block_count)
@@ -97,14 +97,13 @@
                             x[slot[first + s], :, columns] = part[s * comps : (s + 1) * comps]
 
 
-def project(piece, pieces, kp, blocks, me, row_of, cond, screened):
+def project(start, span, width, kp, blocks, me, row_of, cond, screened):
     pair_count, comps, rows = cond.shape
-    block_count, _, cols = screened.shape
+    block_count = screened.shape[0]
     cap = 3 * pair_count // 8
-    span = cols // pieces
-    halves = 2
+    halves = span // width
     return pl.pallas_call(
-        functools.partial(project_kernel, cap, kp, piece),
+        functools.partial(project_kernel, cap, kp, start),
         out_shape=jax.ShapeDtypeStruct((pair_count, comps, span), cond.dtype),
         in_specs=[
             pl.BlockSpec(memory_space=pltpu.SMEM),
@@ -120,7 +119,7 @@
             pltpu.VMEM((block_count, rows, span), screened.dtype),
             pltpu.SemaphoreType.DMA((block_count, halves)),
         ],
-        compiler_params=pltpu.CompilerParams(vmem_limit_bytes=24 << 20),
+        compiler_params=pltpu.CompilerParams(vmem_limit_bytes=32 << 20),
         cost_estimate=pl.CostEstimate(
             flops=2 * pair_count * comps * rows * span,
             bytes_accessed=2 * (block_count * rows * span + pair_count * comps * (rows + span)),
@@ -133,7 +132,7 @@
 def contract_kernel(kp, parts, n, row_of, col_of, *refs):
     xs, vale = refs[: -n - 1], refs[-n - 1 : -1]
     out = refs[-1]
-    comps, width = xs[0].shape[1:]
+    comps = xs[0].shape[1]
     k_count = xs[0].shape[0] // kp
     rows = vale[0].shape[0] // k_count
     total = n * rows
@@ -151,9 +150,12 @@
     picked = []
     for k in range(k_count):
         acc = jnp.zeros((kp * comps, total), jnp.float32)
-        for t, x in enumerate(xs):
+        start = 0
+        for x in xs:
+            width = x.shape[2]
             left = x[k * kp : (k + 1) * kp].reshape(kp * comps, width)
-            right = jnp.concatenate([v[k * rows : (k + 1) * rows, t * width : (t + 1) * width] for v in vale], axis=0)
+            right = jnp.concatenate([v[k * rows : (k + 1) * rows, start : start + width] for v in vale], axis=0)
+            start += width
             acc += lax.dot_general(left, right, (((1,), (1,)), ((), ())), preferred_element_type=jnp.float32)
         one = jnp.zeros((comps, total), jnp.float32)
         for j in range(kp):
@@ -214,8 +216,10 @@
     me = (c * (k_count // m)).reshape(1)
 
     xs = []
-    for piece in range(PIECES):
-        xs.append(project(piece, PIECES, kp, pair_block, me, w.reshape(1), cond, screened))
+    unit = cols // sum(SPANS)
+    for piece, size in enumerate(SPANS):
+        start = unit * sum(SPANS[:piece])
+        xs.append(project(start, unit * size, unit, kp, pair_block, me, w.reshape(1), cond, screened))
 
     parts = n // C
     width = V * V // parts

time: 99.7 us -> 99.7 us (level)
  no operation moved by 1% of the time
where the time goes in v3:
time: 99.7 us; the launch traced here: 99.5 us
  Pallas kernels  34.8 us (35%)
  waiting for transfers between devices  27.9 us (28%)
  starting transfers between devices  20.6 us (21%)
  blocking collectives  12.8 us (13%)
  local copies, waits for them, and re-layouts  2.01 us (2%)
  other arithmetic  1.33 us (1%)
    pallas_call x4, Pallas kernels, project(): pl.pallas_call(functools.partial(project_kernel, cap, kp, start), out_sha...  30.2 us
    ppermute x16, waiting for transfers between devices, move(): return lax.ppermute(array, AXES, pairs_of(n, m, to, across))  27.9 us
    ppermute x16, starting transfers between devices, move(): return lax.ppermute(array, AXES, pairs_of(n, m, to, across))  20.6 us
    all_to_all x1, blocking collectives, direct_kernel(): got = lax.all_to_all(sent, AXES, 0, 0, tiled=True)  12.8 us
    pallas_call x1, Pallas kernels, contract(): pl.pallas_call(functools.partial(contract_kernel, kp, parts, n), out_shap...  4.59 us
  transfers between devices with their start and end apart: 16, of which 2 were waited for; matrix products, arithmetic and copies ran while one was open for 1% of the time, Pallas kernels for 30%

profile of v3, /device:TPU:0, one launch (start us, length us, event | category | flops | bytes accessed | tf_op | source)
XLA Modules:
  0.0 99.5 jit_solution(3122084588673675544)
XLA Ops:
  0.0 1.2 %reshape.30.refs_4_ = bf16[32,8192]{1,0:T(8,128)(2,1)S(1)} reshape(bf16[2,4,4,8192]{3,2,1,0:T(4,128)(2,1)} %param.5) | data formatting | bytes 1048576 | tf_op jit(solution)/shard_map/reshape | solution.py:210
  1.2 4.1 %collective-permute-start.8 = (bf16[32,8192]{1,0:T(8,128)(2,1)S(1)}, bf16[32,8192]{1,0:T(8,128)(2,1)S(1)}, u32[]{:S(2)}, u32[]{:S(2)}) collective-permute-start(bf16[32,8192]{1,0:T(8,128)(2,1)S(1)} %reshape.30.refs_4_), channel_id=1, source_target_pairs={{0,16},{1,17},{2,18},{3,19},{4,20},{5,21},{6,22},{7,23},{8,24},{9,... | collective-permute-start | bytes 1572872 | tf_op jit(solution)/shard_map/ppermute | solution.py:24
  5.3 1.5 %collective-permute-start.1 = (bf16[32,8192]{1,0:T(8,128)(2,1)S(1)}, bf16[32,8192]{1,0:T(8,128)(2,1)S(1)}, u32[]{:S(2)}, u32[]{:S(2)}) collective-permute-start(bf16[32,8192]{1,0:T(8,128)(2,1)S(1)} %reshape.30.refs_4_), channel_id=1, source_target_pairs={{0,2},{1,5},{2,0},{3,7},{4,6},{5,1},{6,4},{7,3},{8,10},{9,13},{10,... | collective-permute-start | bytes 1572872 | tf_op jit(solution)/shard_map/ppermute | solution.py:24
  6.8 1.6 %collective-permute-start.4 = (bf16[32,8192]{1,0:T(8,128)(2,1)S(1)}, bf16[32,8192]{1,0:T(8,128)(2,1)S(1)}, u32[]{:S(2)}, u32[]{:S(2)}) collective-permute-start(bf16[32,8192]{1,0:T(8,128)(2,1)S(1)} %reshape.30.refs_4_), channel_id=1, source_target_pairs={{0,8},{1,9},{2,10},{3,11},{4,12},{5,13},{6,14},{7,15},{8,0},{9,1},... | collective-permute-start | bytes 1572872 | tf_op jit(solution)/shard_map/ppermute | solution.py:24
  8.4 1.5 %collective-permute-start.2 = (bf16[32,8192]{1,0:T(8,128)(2,1)S(1)}, bf16[32,8192]{1,0:T(8,128)(2,1)S(1)}, u32[]{:S(2)}, u32[]{:S(2)}) collective-permute-start(bf16[32,8192]{1,0:T(8,128)(2,1)S(1)} %reshape.30.refs_4_), channel_id=1, source_target_pairs={{0,4},{1,3},{2,6},{3,1},{4,0},{5,7},{6,2},{7,5},{8,12},{9,11},{10,... | collective-permute-start | bytes 1572872 | tf_op jit(solution)/shard_map/ppermute | solution.py:24
  9.9 18.7 %collective-permute-done.8.refs_12_ = bf16[32,8192]{1,0:T(8,128)(2,1)S(1)} collective-permute-done((bf16[32,8192]{1,0:T(8,128)(2,1)S(1)}, bf16[32,8192]{1,0:T(8,128)(2,1)S(1)}, u32[]{:S(2)}, u32[]{:S(2)}) %collective-permute-start.8) | collective-permute-done | bytes 524320 | tf_op jit(solution)/shard_map/ppermute | solution.py:24
  28.6 0.7 collective-permute-start.12
  29.2 1.5 %collective-permute-start.9 = (bf16[32,8192]{1,0:T(8,128)(2,1)S(1)}, bf16[32,8192]{1,0:T(8,128)(2,1)}, u32[]{:S(2)}, u32[]{:S(2)}) collective-permute-start(bf16[32,8192]{1,0:T(8,128)(2,1)S(1)} %collective-permute-done.8.refs_12_), channel_id=1, source_target_pairs={{0,2},{1,5},{2,0},{3,7},{4,6},{5,1},{6,4},{7,3},{8,10},{9,13},{10,... | collective-permute-start | bytes 1572872 | tf_op jit(solution)/shard_map/ppermute | solution.py:24
  30.7 1.5 %collective-permute-start.3 = (bf16[32,8192]{1,0:T(8,128)(2,1)S(1)}, bf16[32,8192]{1,0:T(8,128)(2,1)}, u32[]{:S(2)}, u32[]{:S(2)}) collective-permute-start(bf16[32,8192]{1,0:T(8,128)(2,1)S(1)} %collective-permute-done.1.refs_5_), channel_id=1, source_target_pairs={{0,4},{1,3},{2,6},{3,1},{4,0},{5,7},{6,2},{7,5},{8,12},{9,11},{10,... | collective-permute-start | bytes 1572872 | tf_op jit(solution)/shard_map/ppermute | solution.py:24
  32.8 1.4 %collective-permute-start.5 = (bf16[32,8192]{1,0:T(8,128)(2,1)S(1)}, bf16[32,8192]{1,0:T(8,128)(2,1)}, u32[]{:S(2)}, u32[]{:S(2)}) collective-permute-start(bf16[32,8192]{1,0:T(8,128)(2,1)S(1)} %collective-permute-done.1.refs_5_), channel_id=1, source_target_pairs={{0,8},{1,9},{2,10},{3,11},{4,12},{5,13},{6,14},{7,15},{8,0},{9,1},... | collective-permute-start | bytes 1572872 | tf_op jit(solution)/shard_map/ppermute | solution.py:24
  34.2 9.2 %collective-permute-done.12.refs_16_ = bf16[32,8192]{1,0:T(8,128)(2,1)S(1)} collective-permute-done((bf16[32,8192]{1,0:T(8,128)(2,1)S(1)}, bf16[32,8192]{1,0:T(8,128)(2,1)S(1)}, u32[]{:S(2)}, u32[]{:S(2)}) %collective-permute-start.12) | collective-permute-done | bytes 524320 | tf_op jit(solution)/shard_map/ppermute | solution.py:24
  43.4 1.5 %collective-permute-start.13 = (bf16[32,8192]{1,0:T(8,128)(2,1)S(1)}, bf16[32,8192]{1,0:T(8,128)(2,1)}, u32[]{:S(2)}, u32[]{:S(2)}) collective-permute-start(bf16[32,8192]{1,0:T(8,128)(2,1)S(1)} %collective-permute-done.12.refs_16_), channel_id=1, source_target_pairs={{0,2},{1,5},{2,0},{3,7},{4,6},{5,1},{6,4},{7,3},{8,10},{9,13},{10,... | collective-permute-start | bytes 1572872 | tf_op jit(solution)/shard_map/ppermute | solution.py:24
  44.9 1.3 %pad_maximum_fusion = bf16[2,4,64,1024]{3,2,1,0:T(8,128)(2,1)S(1)} fusion(bf16[1,4,64,1024]{3,2,1,0:T(8,128)(2,1)} %copy-done.1, bf16[1,4,64,1024]{3,2,1,0:T(8,128)(2,1)} %param.4), kind=kLoop, calls=%fused_computation | loop fusion | flops 524288 | bytes 2097152 | tf_op jit(solution)/shard_map/concatenate | solution.py:215
  46.2 7.5 %project.6.refs_2_ = bf16[8,64,2048]{2,1,0:T(8,128)(2,1)S(1)} custom-call(s32[2,4]{1,0:T(2,128)S(1)} %copy-done, s32[1]{0:T(128)} %bitcast.1.me.col_of, s32[1]{0:T(128)} %bitcast.row_of, bf16[8,64,1024]{2,1,0:T(8,128)(2,1)S(1)} %bitcast.7, bf16[4,1024,8192]{2,1,0:T(8,128)(2,1)} %w.7), custom_call_target="tpu_custom_call" | custom-call | flops 2147483648 | bytes 19922944 | tf_op jit(solution)/shard_map/project/pallas_call | solution.py:105
  53.8 1.6 %collective-permute-start.6 = (bf16[32,8192]{1,0:T(8,128)(2,1)S(1)}, bf16[32,8192]{1,0:T(8,128)(2,1)S(1)}, u32[]{:S(2)}, u32[]{:S(2)}) collective-permute-start(bf16[32,8192]{1,0:T(8,128)(2,1)S(1)} %collective-permute-done.4.refs_8_), channel_id=1, source_target_pairs={{0,4},{1,3},{2,6},{3,1},{4,0},{5,7},{6,2},{7,5},{8,12},{9,11},{10,... | collective-permute-start | bytes 1572872 | tf_op jit(solution)/shard_map/ppermute | solution.py:24
  55.9 1.5 %collective-permute-start.11 = (bf16[32,8192]{1,0:T(8,128)(2,1)}, bf16[32,8192]{1,0:T(8,128)(2,1)S(1)}, u32[]{:S(2)}, u32[]{:S(2)}) collective-permute-start(bf16[32,8192]{1,0:T(8,128)(2,1)} %collective-permute-done.9.refs_13_), channel_id=1, source_target_pairs={{0,4},{1,3},{2,6},{3,1},{4,0},{5,7},{6,2},{7,5},{8,12},{9,11},{10,... | collective-permute-start | bytes 1572872 | tf_op jit(solution)/shard_map/ppermute | solution.py:24
  57.4 0.6 collective-permute-start.7
  58.0 0.5 collective-permute-start.15
  58.5 5.0 %project.5.refs_1_ = bf16[8,64,1024]{2,1,0:T(8,128)(2,1)S(1)} custom-call(s32[2,4]{1,0:T(2,128)S(1)} %copy-done, s32[1]{0:T(128)} %bitcast.1.me.col_of, s32[1]{0:T(128)} %bitcast.row_of, bf16[8,64,1024]{2,1,0:T(8,128)(2,1)S(1)} %bitcast.8, bf16[4,1024,8192]{2,1,0:T(8,128)(2,1)} %w.7), custom_call_target="tpu_custom_call" | custom-call | flops 1073741824 | bytes 10485760 | tf_op jit(solution)/shard_map/project/pallas_call | solution.py:105
  63.5 7.5 %project.7.refs_3_ = bf16[8,64,2048]{2,1,0:T(8,128)(2,1)S(1)} custom-call(s32[2,4]{1,0:T(2,128)S(1)} %copy-done, s32[1]{0:T(128)} %bitcast.1.me.col_of, s32[1]{0:T(128)} %bitcast.row_of, bf16[8,64,1024]{2,1,0:T(8,128)(2,1)S(1)} %bitcast.9, bf16[4,1024,8192]{2,1,0:T(8,128)(2,1)} %w.7), custom_call_target="tpu_custom_call" | custom-call | flops 2147483648 | bytes 19922944 | tf_op jit(solution)/shard_map/project/pallas_call | solution.py:105
  71.0 10.1 %project.4.refs_0_ = bf16[8,64,3072]{2,1,0:T(8,128)(2,1)S(1)} custom-call(s32[2,4]{1,0:T(2,128)S(1)} %copy-done, s32[1]{0:T(128)} %bitcast.1.me.col_of, s32[1]{0:T(128)} %bitcast.row_of, bf16[8,64,1024]{2,1,0:T(8,128)(2,1)S(1)} %bitcast.10, bf16[4,1024,8192]{2,1,0:T(8,128)(2,1)} %w.7), custom_call_target="tpu_custom_call" | custom-call | flops 3221225472 | bytes 29360128 | tf_op jit(solution)/shard_map/project/pallas_call | solution.py:105
  81.2 4.6 %contract.1 = f32[16,2,8,128]{3,2,1,0:T(8,128)S(1)} custom-call(s32[1]{0:T(128)} %bitcast.row_of, s32[1]{0:T(128)} %bitcast.1.me.col_of, bf16[8,64,3072]{2,1,0:T(8,128)(2,1)S(1)} %project.4.refs_0_, bf16[8,64,1024]{2,1,0:T(8,128)(2,1)S(1)} %project.5.refs_1_, bf16[8,64,2048]{2,1,0:T(8,128)(2,1)S(1)} %project.6.refs_2_, ...), custom_call_target="tpu_custom_call" | custom-call | flops 2147483648 | bytes 16777216 | tf_op jit(solution)/shard_map/contract/pallas_call | solution.py:182
  85.8 12.8 %all_to_all.5 = f32[32,8,128]{2,1,0:T(8,128)S(1)} all-to-all(f32[32,8,128]{2,1,0:T(8,128)S(1)} %bitcast.11), channel_id=1, replica_groups=mesh['wrow'=16,'kblk'=2] {'wrow','kblk'}, dimensions={0} | all-to-all | bytes 262144 | tf_op jit(solution)/shard_map/all_to_all | solution.py:229
  98.8 0.7 reshape.32
  (24 shorter events, 1.2 us)
Async XLA Ops:
  0.0 46.2 %copy-start = (s32[2,4]{1,0:T(2,128)S(1)}, s32[2,4]{1,0:T(2,128)}, u32[]{:S(2)}) copy-start(s32[2,4]{1,0:T(2,128)} %blocks.7) | copy-start | bytes 100
  1.2 27.4 %collective-permute-start.8 = (bf16[32,8192]{1,0:T(8,128)(2,1)S(1)}, bf16[32,8192]{1,0:T(8,128)(2,1)S(1)}, u32[]{:S(2)}, u32[]{:S(2)}) collective-permute-start(bf16[32,8192]{1,0:T(8,128)(2,1)S(1)} %reshape.30.refs_4_), channel_id=1, source_target_pairs={{0,16},{1,17},{2,18},{3,19},{4,20},{5,21},{6,22},{7,23},{8,24},{9,... | collective-permute-start | bytes 1572872 | tf_op jit(solution)/shard_map/ppermute | solution.py:24
  5.3 23.9 %collective-permute-start = (bf16[1,4,64,1024]{3,2,1,0:T(8,128)(2,1)}, bf16[1,4,64,1024]{3,2,1,0:T(8,128)(2,1)S(1)}, u32[]{:S(2)}, u32[]{:S(2)}) collective-permute-start(bf16[1,4,64,1024]{3,2,1,0:T(8,128)(2,1)} %param.4), channel_id=1, source_target_pairs={{0,1},{1,0},{2,3},{3,2},{4,5},{5,4},{6,7},{7,6},{8,9},{9,8},{10,11... | collective-permute-start | bytes 1572872 | tf_op jit(solution)/shard_map/ppermute | solution.py:24
  5.3 25.4 %collective-permute-start.1 = (bf16[32,8192]{1,0:T(8,128)(2,1)S(1)}, bf16[32,8192]{1,0:T(8,128)(2,1)S(1)}, u32[]{:S(2)}, u32[]{:S(2)}) collective-permute-start(bf16[32,8192]{1,0:T(8,128)(2,1)S(1)} %reshape.30.refs_4_), channel_id=1, source_target_pairs={{0,2},{1,5},{2,0},{3,7},{4,6},{5,1},{6,4},{7,3},{8,10},{9,13},{10,... | collective-permute-start | bytes 1572872 | tf_op jit(solution)/shard_map/ppermute | solution.py:24
  6.8 25.5 %collective-permute-start.4 = (bf16[32,8192]{1,0:T(8,128)(2,1)S(1)}, bf16[32,8192]{1,0:T(8,128)(2,1)S(1)}, u32[]{:S(2)}, u32[]{:S(2)}) collective-permute-start(bf16[32,8192]{1,0:T(8,128)(2,1)S(1)} %reshape.30.refs_4_), channel_id=1, source_target_pairs={{0,8},{1,9},{2,10},{3,11},{4,12},{5,13},{6,14},{7,15},{8,0},{9,1},... | collective-permute-start | bytes 1572872 | tf_op jit(solution)/shard_map/ppermute | solution.py:24
  8.4 24.4 %collective-permute-start.2 = (bf16[32,8192]{1,0:T(8,128)(2,1)S(1)}, bf16[32,8192]{1,0:T(8,128)(2,1)S(1)}, u32[]{:S(2)}, u32[]{:S(2)}) collective-permute-start(bf16[32,8192]{1,0:T(8,128)(2,1)S(1)} %reshape.30.refs_4_), channel_id=1, source_target_pairs={{0,4},{1,3},{2,6},{3,1},{4,0},{5,7},{6,2},{7,5},{8,12},{9,11},{10,... | collective-permute-start | bytes 1572872 | tf_op jit(solution)/shard_map/ppermute | solution.py:24
  28.6 14.8 %collective-permute-start.12 = (bf16[32,8192]{1,0:T(8,128)(2,1)S(1)}, bf16[32,8192]{1,0:T(8,128)(2,1)S(1)}, u32[]{:S(2)}, u32[]{:S(2)}) collective-permute-start(bf16[32,8192]{1,0:T(8,128)(2,1)S(1)} %collective-permute-done.8.refs_12_), channel_id=1, source_target_pairs={{0,8},{1,9},{2,10},{3,11},{4,12},{5,13},{6,14},{7,15},{8,0},{9,1},... | collective-permute-start | bytes 1572872 | tf_op jit(solution)/shard_map/ppermute | solution.py:24
  29.2 14.1 %copy-start.1 = (bf16[1,4,64,1024]{3,2,1,0:T(8,128)(2,1)}, bf16[1,4,64,1024]{3,2,1,0:T(8,128)(2,1)S(1)}, u32[]{:S(2)}) copy-start(bf16[1,4,64,1024]{3,2,1,0:T(8,128)(2,1)S(1)} %collective-permute-done) | copy-start | bytes 1572868
  29.2 24.5 %collective-permute-start.9 = (bf16[32,8192]{1,0:T(8,128)(2,1)S(1)}, bf16[32,8192]{1,0:T(8,128)(2,1)}, u32[]{:S(2)}, u32[]{:S(2)}) collective-permute-start(bf16[32,8192]{1,0:T(8,128)(2,1)S(1)} %collective-permute-done.8.refs_12_), channel_id=1, source_target_pairs={{0,2},{1,5},{2,0},{3,7},{4,6},{5,1},{6,4},{7,3},{8,10},{9,13},{10,... | collective-permute-start | bytes 1572872 | tf_op jit(solution)/shard_map/ppermute | solution.py:24
  30.7 24.6 %collective-permute-start.3 = (bf16[32,8192]{1,0:T(8,128)(2,1)S(1)}, bf16[32,8192]{1,0:T(8,128)(2,1)}, u32[]{:S(2)}, u32[]{:S(2)}) collective-permute-start(bf16[32,8192]{1,0:T(8,128)(2,1)S(1)} %collective-permute-done.1.refs_5_), channel_id=1, source_target_pairs={{0,4},{1,3},{2,6},{3,1},{4,0},{5,7},{6,2},{7,5},{8,12},{9,11},{10,... | collective-permute-start | bytes 1572872 | tf_op jit(solution)/shard_map/ppermute | solution.py:24
  32.3 23.6 %collective-permute-start.10 = (bf16[32,8192]{1,0:T(8,128)(2,1)S(1)}, bf16[32,8192]{1,0:T(8,128)(2,1)}, u32[]{:S(2)}, u32[]{:S(2)}) collective-permute-start(bf16[32,8192]{1,0:T(8,128)(2,1)S(1)} %collective-permute-done.8.refs_12_), channel_id=1, source_target_pairs={{0,4},{1,3},{2,6},{3,1},{4,0},{5,7},{6,2},{7,5},{8,12},{9,11},{10,... | collective-permute-start | bytes 1572872 | tf_op jit(solution)/shard_map/ppermute | solution.py:24
  32.8 24.6 %collective-permute-start.5 = (bf16[32,8192]{1,0:T(8,128)(2,1)S(1)}, bf16[32,8192]{1,0:T(8,128)(2,1)}, u32[]{:S(2)}, u32[]{:S(2)}) collective-permute-start(bf16[32,8192]{1,0:T(8,128)(2,1)S(1)} %collective-permute-done.1.refs_5_), channel_id=1, source_target_pairs={{0,8},{1,9},{2,10},{3,11},{4,12},{5,13},{6,14},{7,15},{8,0},{9,1},... | collective-permute-start | bytes 1572872 | tf_op jit(solution)/shard_map/ppermute | solution.py:24
  43.4 14.6 %collective-permute-start.13 = (bf16[32,8192]{1,0:T(8,128)(2,1)S(1)}, bf16[32,8192]{1,0:T(8,128)(2,1)}, u32[]{:S(2)}, u32[]{:S(2)}) collective-permute-start(bf16[32,8192]{1,0:T(8,128)(2,1)S(1)} %collective-permute-done.12.refs_16_), channel_id=1, source_target_pairs={{0,2},{1,5},{2,0},{3,7},{4,6},{5,1},{6,4},{7,3},{8,10},{9,13},{10,... | collective-permute-start | bytes 1572872 | tf_op jit(solution)/shard_map/ppermute | solution.py:24
  53.8 27.4 %collective-permute-start.6 = (bf16[32,8192]{1,0:T(8,128)(2,1)S(1)}, bf16[32,8192]{1,0:T(8,128)(2,1)S(1)}, u32[]{:S(2)}, u32[]{:S(2)}) collective-permute-start(bf16[32,8192]{1,0:T(8,128)(2,1)S(1)} %collective-permute-done.4.refs_8_), channel_id=1, source_target_pairs={{0,4},{1,3},{2,6},{3,1},{4,0},{5,7},{6,2},{7,5},{8,12},{9,11},{10,... | collective-permute-start | bytes 1572872 | tf_op jit(solution)/shard_map/ppermute | solution.py:24
  55.4 25.8 %collective-permute-start.14 = (bf16[32,8192]{1,0:T(8,128)(2,1)S(1)}, bf16[32,8192]{1,0:T(8,128)(2,1)S(1)}, u32[]{:S(2)}, u32[]{:S(2)}) collective-permute-start(bf16[32,8192]{1,0:T(8,128)(2,1)S(1)} %collective-permute-done.12.refs_16_), channel_id=1, source_target_pairs={{0,4},{1,3},{2,6},{3,1},{4,0},{5,7},{6,2},{7,5},{8,12},{9,11},{10,... | collective-permute-start | bytes 1572872 | tf_op jit(solution)/shard_map/ppermute | solution.py:24
  55.9 25.3 %collective-permute-start.11 = (bf16[32,8192]{1,0:T(8,128)(2,1)}, bf16[32,8192]{1,0:T(8,128)(2,1)S(1)}, u32[]{:S(2)}, u32[]{:S(2)}) collective-permute-start(bf16[32,8192]{1,0:T(8,128)(2,1)} %collective-permute-done.9.refs_13_), channel_id=1, source_target_pairs={{0,4},{1,3},{2,6},{3,1},{4,0},{5,7},{6,2},{7,5},{8,12},{9,11},{10,... | collective-permute-start | bytes 1572872 | tf_op jit(solution)/shard_map/ppermute | solution.py:24
  57.4 23.8 %collective-permute-start.7 = (bf16[32,8192]{1,0:T(8,128)(2,1)}, bf16[32,8192]{1,0:T(8,128)(2,1)S(1)}, u32[]{:S(2)}, u32[]{:S(2)}) collective-permute-start(bf16[32,8192]{1,0:T(8,128)(2,1)} %collective-permute-done.3.refs_7_), channel_id=1, source_target_pairs={{0,8},{1,9},{2,10},{3,11},{4,12},{5,13},{6,14},{7,15},{8,0},{9,1},... | collective-permute-start | bytes 1572872 | tf_op jit(solution)/shard_map/ppermute | solution.py:24
  58.0 23.2 %collective-permute-start.15 = (bf16[32,8192]{1,0:T(8,128)(2,1)}, bf16[32,8192]{1,0:T(8,128)(2,1)S(1)}, u32[]{:S(2)}, u32[]{:S(2)}) collective-permute-start(bf16[32,8192]{1,0:T(8,128)(2,1)} %collective-permute-done.13.refs_17_), channel_id=1, source_target_pairs={{0,4},{1,3},{2,6},{3,1},{4,0},{5,7},{6,2},{7,5},{8,12},{9,11},{10,... | collective-permute-start | bytes 1572872 | tf_op jit(solution)/shard_map/ppermute | solution.py:24
